TPU v7x, 512 devices: a whole 4x8x8 slice. The times are simulated.
512 devices in a mesh: ctx: 64 (over z, y), tp: 8 (over x, core).
Axes of the slice: x: 4, y: 8, z: 8, core: 2. Of those that a mesh axis runs over, the one named last changes fastest.
Arguments:
- span_q: bfloat16 [8192, 8192], P('ctx', 'tp'), may hold values from -21 to 21
- span_kv: bfloat16 [2, 8192, 1024], P(None, 'ctx', 'tp'), may hold values from -20 to 20
- cache_kv: bfloat16 [2, 65536, 1024], P(None, 'ctx', 'tp'), may hold values from -20 to 20
- anchor_kv: bfloat16 [2, 2048, 1024], P(None, 'ctx', 'tp'), may hold values from -20 to 20
- block_len: int32 [64], P('ctx'), may hold values from 1 to 1024, 40960 in all
- queries: bfloat16 [128, 8192], P('ctx', 'tp'), may hold values from -21 to 21
- out_weight: bfloat16 [8192, 8192], P('tp', 'ctx'), may hold values from -0.0625 to 0.0625
Outputs:
- span_out: bfloat16 [8192, 8192], P('ctx', 'tp')
- answer: bfloat16 [128, 8192], P('tp', 'ctx')
Inputs may be any that keep to these rules, and one draw needn't show every extreme that they name: The new tokens of block c follow its block_len[c] valid cache rows.
All inputs are finite; a program needn't handle non-finite values.
Results may differ from a plain program's by a relative error of at most 0.0049.
Values may be sent and summed in bfloat16 or wider, within the bound.
A program may use at most 64 MiB of HBM per device.

v0:
```python
import math

import jax
import jax.numpy as jnp
from jax import lax
from jax.sharding import PartitionSpec as P

HD = 128


masked_score = -1e30


def all_heads(query_rows, key_rows, value_rows, visible):
    row_count = query_rows.shape[0]
    head_count = query_rows.shape[1] // HD
    score_scale = 1.0 / math.sqrt(HD)

    def per_head(head_index, running):
        maxima, totals, outputs = running
        q_head = lax.dynamic_slice_in_dim(query_rows, head_index * HD, HD, 1)
        scores = (
            jnp.einsum("qd,nd->qn", q_head, key_rows, preferred_element_type=jnp.float32)
            * score_scale
        )
        scores = jnp.where(visible, scores, masked_score)
        peak_score = jnp.max(scores, axis=1, keepdims=True)
        weights = jnp.exp(scores - peak_score)
        weight_sum = jnp.sum(weights, axis=1, keepdims=True)
        product = jnp.einsum(
            "qn,nd->qd",
            weights.astype(jnp.bfloat16),
            value_rows,
            preferred_element_type=jnp.float32,
        )
        maxima = lax.dynamic_update_slice_in_dim(maxima, peak_score, head_index, 1)
        totals = lax.dynamic_update_slice_in_dim(totals, weight_sum, head_index, 1)
        outputs = lax.dynamic_update_slice_in_dim(outputs, product, head_index * HD, 1)
        return (maxima, totals, outputs)

    initial = (
        jnp.zeros((row_count, head_count), jnp.float32),
        jnp.zeros((row_count, head_count), jnp.float32),
        jnp.zeros((row_count, head_count * HD), jnp.float32),
    )
    return lax.fori_loop(0, head_count, per_head, initial)


def local(span_q, span_kv, cache_kv, anchor_kv, block_len, queries, out_weight):
    cache_count = cache_kv.shape[1]
    span_count = span_kv.shape[1]
    length = block_len[0]
    local_kv = jnp.concatenate([cache_kv, span_kv], axis=1)
    anchor_all = lax.all_gather(anchor_kv, "ctx", axis=1, tiled=True)
    query_all = lax.all_gather(queries, "ctx", axis=0, tiled=True)
    anchor_count = anchor_all.shape[1]
    first_kv = jnp.concatenate([anchor_all, local_kv], axis=1)
    key_total = first_kv.shape[1]
    column = lax.broadcasted_iota(jnp.int32, (span_count, key_total), 1)
    query_pos = lax.broadcasted_iota(jnp.int32, (span_count, key_total), 0)
    in_cache = (column >= anchor_count) & (column < anchor_count + cache_count)
    in_span = column >= anchor_count + cache_count
    visible = jnp.where(
        in_cache,
        column - anchor_count < length,
        jnp.where(in_span, column - anchor_count - cache_count <= query_pos, True),
    )
    first_max, first_sum, first_values = all_heads(span_q, first_kv[0], first_kv[1], visible)
    span_out = (first_values / jnp.repeat(first_sum, HD, axis=1)).astype(jnp.bfloat16)
    own_count = anchor_kv.shape[1]
    second_kv = jnp.concatenate([anchor_kv, local_kv], axis=1)
    column_two = lax.broadcasted_iota(jnp.int32, (1, second_kv.shape[1]), 1)
    cache_two = (column_two >= own_count) & (column_two < own_count + cache_count)
    visible_two = jnp.where(cache_two, column_two - own_count < length, True)
    part_max, part_sum, part_values = all_heads(query_all, second_kv[0], second_kv[1], visible_two)
    global_max = lax.pmax(part_max, "ctx")
    rescale = jnp.exp(part_max - global_max)
    full_sum, full_values = lax.psum(
        (part_sum * rescale, part_values * jnp.repeat(rescale, HD, axis=1)), "ctx"
    )
    attended = (full_values / jnp.repeat(full_sum, HD, axis=1)).astype(jnp.bfloat16)
    partial_value = jnp.dot(attended, out_weight, preferred_element_type=jnp.float32)
    answer = lax.psum_scatter(partial_value, "tp", scatter_dimension=0, tiled=True).astype(
        jnp.bfloat16
    )
    return (span_out, answer)


def solution(mesh):
    placed = (
        P("ctx", "tp"),
        P(None, "ctx", "tp"),
        P(None, "ctx", "tp"),
        P(None, "ctx", "tp"),
        P("ctx"),
        P("ctx", "tp"),
        P("tp", "ctx"),
    )
    return jax.shard_map(
        local,
        mesh=mesh,
        in_specs=placed,
        out_specs=(P("ctx", "tp"), P("tp", "ctx")),
        check_vma=False,
    )
```

profile of v0, /device:TPU:1, one launch (start us, length us, event | category | flops | bytes accessed | tf_op | source)
XLA Modules:
  0.0 452.3 jit_solution(17501054155772972104)
XLA Ops:
  7.2 0.7 all-gather.3.cloned.1.call-update
  8.0 45.7 %all-gather = bf16[64,2,1024]{2,1,0:T(2,128)(2,1)S(1)} all-gather(bf16[1,2,1024]{2,1,0:T(2,128)(2,1)} %bitcast.53), channel_id=1, replica_groups=mesh['ctx'=64,'tp'=8] {'ctx'}, dimensions={0}, use_global_device_ids=true | all-gather | bytes 266240 | tf_op jit(solution)/shard_map/all_gather | solution.py:55
  54.5 0.7 constant_dynamic-update-slice_fusion.5
  55.2 0.6 iota_add_fusion
  55.8 35.5 %all-gather.3.cloned.1.call-done = bf16[2,2048,128]{2,1,0:T(8,128)(2,1)} async-done(((bf16[2,32,128]{2,1,0:T(8,128)(2,1)}), bf16[2,2048,128]{2,1,0:T(8,128)(2,1)}) %all-gather.3.cloned.1.call-update) | async-done | bytes 1048592 | tf_op jit(solution)/shard_map/all_gather | solution.py:54
  91.3 1.3 constant_dynamic-update-slice_fusion.2
  92.9 0.8 copy-done.1
  93.7 1.1 slice_bitcast_fusion.2
  94.9 13.0 %while.35 = (s32[]{:T(128)}, f32[128,8]{0,1:T(8,128)S(1)}, f32[128,8]{0,1:T(8,128)S(1)}, f32[128,1024]{1,0:T(8,128)S(1)}, bf16[128,1024]{1,0:T(8,128)(2,1)S(1)},...) while((s32[]{:T(128)}, f32[128,8]{0,1:T(8,128)S(1)}, ...), condition=%wide.region_7.8_spmd.clone, body=%wide.region_4.7_spmd.clone.sunk | while | flops 78662336 | bytes 2530647 | solution.py:46
  94.9 0.7 select_reduce_fusion.2
  95.6 0.4 fusion.51
  96.5 0.7 select_reduce_fusion.2
  97.2 0.4 fusion.51
  97.6 0.3 convolution_dynamic-update-slice_fusion.5
  98.1 0.7 select_reduce_fusion.2
  98.8 0.4 fusion.51
  99.2 0.3 convolution_dynamic-update-slice_fusion.5
  99.8 0.7 select_reduce_fusion.2
  100.5 0.4 fusion.51
  100.8 0.3 convolution_dynamic-update-slice_fusion.5
  101.4 0.7 select_reduce_fusion.2
  102.1 0.4 fusion.51
  102.4 0.3 convolution_dynamic-update-slice_fusion.5
  103.0 0.7 select_reduce_fusion.2
  103.7 0.4 fusion.51
  104.1 0.3 convolution_dynamic-update-slice_fusion.5
  104.6 0.7 select_reduce_fusion.2
  105.3 0.4 fusion.51
  106.3 0.7 select_reduce_fusion.2
  106.9 0.4 fusion.51
  107.3 0.3 convolution_dynamic-update-slice_fusion.5
  107.9 113.5 %pmax.7 = f32[128,8]{0,1:T(8,128)S(1)} all-reduce(f32[128,8]{0,1:T(8,128)S(1)} %get-tuple-element.271), channel_id=1, replica_groups=mesh['ctx'=64,'tp'=8] {'ctx'}, use_global_device_ids=true, to_apply=%region_8.9 | all-reduce | flops 1024 | bytes 8192 | tf_op jit(solution)/shard_map/pmax | solution.py:76
  221.7 0.9 bitcast_multiply_fusion
  222.9 19.4 %while.34 = (s32[]{:T(128)}, f32[128,8]{0,1:T(8,128)S(1)}, f32[128,1024]{1,0:T(8,128)S(1)}, bf16[128,1024]{1,0:T(8,128)(2,1)}, bf16[3200,128]{1,0:T(8,128)(2,1)S...) while((s32[]{:T(128)}, f32[128,8]{0,1:T(8,128)S(1)}, ...), condition=%wide.region_3.4_spmd.clone, body=%wide.region_0.3_spmd.clone.sunk | while | flops 213810944 | bytes 6681151 | solution.py:46
  222.9 1.5 fusion.46
  224.4 0.5 convolution_dynamic-update-slice_fusion.4
  224.9 0.4 fusion.47
  225.3 1.5 fusion.46
  226.9 0.5 convolution_dynamic-update-slice_fusion.4
  227.3 0.4 fusion.47
  227.8 1.5 fusion.46
  229.3 0.5 convolution_dynamic-update-slice_fusion.4
  229.8 0.4 fusion.47
  230.2 1.5 fusion.46
  231.7 0.5 convolution_dynamic-update-slice_fusion.4
  232.2 0.4 fusion.47
  232.6 1.5 fusion.46
  234.1 0.5 convolution_dynamic-update-slice_fusion.4
  234.6 0.4 fusion.47
  235.0 1.5 fusion.46
  236.6 0.5 convolution_dynamic-update-slice_fusion.4
  237.0 0.4 fusion.47
  237.4 1.5 fusion.46
  239.0 0.5 convolution_dynamic-update-slice_fusion.4
  239.4 0.4 fusion.47
  239.9 1.5 fusion.46
  241.4 0.5 convolution_dynamic-update-slice_fusion.4
  241.9 0.4 fusion.47
  242.3 110.2 %psum.15 = f32[128,8]{0,1:T(8,128)S(1)} all-reduce(f32[128,8]{0,1:T(8,128)S(1)} %get-tuple-element.354), channel_id=1, replica_groups=mesh['ctx'=64,'tp'=8] {'ctx'}, use_global_device_ids=true, to_apply=%region_10.11 | all-reduce | flops 1024 | bytes 8192 | tf_op jit(solution)/shard_map/psum | solution.py:78
  352.6 49.0 %all-reduce.2.cloned.1.call-done = f32[128,1024]{1,0:T(8,128)} async-done(((f32[128,1024]{1,0:T(8,128)}), f32[128,1024]{1,0:T(8,128)}) %all-reduce.2.cloned.1.call-update) | async-done | bytes 524304 | tf_op jit(solution)/shard_map/psum | solution.py:78
  401.9 1.9 fusion.22
  404.0 0.8 fusion.21
  404.8 39.6 %reduce-scatter.2.cloned.1.call-done = f32[16,128]{1,0:T(8,128)} async-done(((f32[128,128]{1,0:T(8,128)}), f32[16,128]{1,0:T(8,128)}) %reduce-scatter.2.cloned.1.call-update) | async-done | bytes 8208 | tf_op jit(solution)/shard_map/reduce_scatter | solution.py:83
  444.5 1.3 convert_element_type.25
  (64 shorter events, 4.4 us)
Async XLA Ops:
  7.2 394.7 %copy-start = (bf16[1024,128]{1,0:T(8,128)(2,1)S(1)}, bf16[1024,128]{1,0:T(8,128)(2,1)}, u32[]{:S(2)}) copy-start(bf16[1024,128]{1,0:T(8,128)(2,1)} %param.17) | copy-start | bytes 786436
  7.2 85.5 %copy-start.2 = (bf16[2,1024,128]{2,1,0:T(8,128)(2,1)S(1)}, bf16[2,1024,128]{2,1,0:T(8,128)(2,1)}, u32[]{:S(2)}) copy-start(bf16[2,1024,128]{2,1,0:T(8,128)(2,1)} %param.13) | copy-start | bytes 1572868
  7.2 84.1 %all-gather.3.cloned.1.call-start = ((), (), s32[]{:S(2)}) async-start(), calls=%async_computation.1 | async-start | bytes 1064960 | tf_op jit(solution)/shard_map/all_gather | solution.py:54
  7.9 393.8 %all-reduce.2.cloned.1.call-start = ((), (), s32[]{:S(2)}) async-start(), calls=%async_computation.2 | async-start | bytes 1048576 | tf_op jit(solution)/shard_map/psum | solution.py:78
  55.8 37.1 %copy-start.3 = (bf16[2,128,128]{2,1,0:T(8,128)(2,1)S(1)}, bf16[2,128,128]{2,1,0:T(8,128)(2,1)}, u32[]{:S(2)}) copy-start(bf16[2,128,128]{2,1,0:T(8,128)(2,1)} %param.12) | copy-start | bytes 196612
  92.9 0.8 copy-start.1
  222.7 221.8 %reduce-scatter.2.cloned.1.call-start = ((), (), s32[]{:S(2)}) async-start(), calls=%async_computation.3 | async-start | bytes 73728 | tf_op jit(solution)/shard_map/reduce_scatter | solution.py:83
Sparse Core Ops, SparseCore 0:
  11.0 80.3 all-gather.2
  222.8 178.8 all-reduce.1
  404.5 39.9 reduce-scatter.1
where the time goes:
time: 454 us; the launch traced here: 452 us
  blocking collectives  269 us (59%)
  waiting for transfers between devices  125 us (28%)
  matrix products  23.1 us (5%)
  between operations  14.6 us (3%)
  other arithmetic  13.6 us (3%)
  local copies, waits for them, and re-layouts  6.12 us (1%)
    pmax x1, blocking collectives, local(): global_max = lax.pmax(part_max, 'ctx')  114 us
    psum x1, blocking collectives, local(): lax.psum((part_sum * rescale, part_values * jnp.repeat(rescale, HD, axis=...  110 us
    psum x1, waiting for transfers between devices, local(): lax.psum((part_sum * rescale, part_values * jnp.repeat(rescale, HD, axis=...  49 us
    all_gather x1, blocking collectives, local(): query_all = lax.all_gather(queries, 'ctx', axis=0, tiled=True)  45.7 us
    reduce_scatter x1, waiting for transfers between devices, local(): lax.psum_scatter(partial_value, 'tp', scatter_dimension=0, tiled=True)  39.6 us
    all_gather x1, waiting for transfers between devices, local(): anchor_all = lax.all_gather(anchor_kv, 'ctx', axis=1, tiled=True)  35.5 us
    dot_general x16, matrix products, per_head(): jnp.einsum('qd,nd->qn', q_head, key_rows, preferred_element_type=jnp.floa...  15.1 us
  transfers between devices with their start and end apart: 3, of which 3 were waited for; matrix products, arithmetic and copies ran while one was open for 5% of the time, Pallas kernels for 0%

commit v1 on v0

v1 whole, which is shorter than its diff:
```python
import math

import jax
import jax.numpy as jnp
from jax import lax
from jax.experimental import pallas as pl
from jax.experimental.pallas import tpu as pltpu
from jax.sharding import PartitionSpec as P

HD = 128
NEG = -1e30
MESH = pl.DeviceIdType.MESH
LOG2 = math.log2(math.e) / math.sqrt(HD)

QA, QB, AB, AA, RO, RL, CO, CL, GB, TP = range(10)


def scores(q, k):
    return lax.dot_general(q, k, (((1,), (1,)), ((), ())), preferred_element_type=jnp.float32)


def softmax_parts(parts, values):
    peak = None
    for s in parts:
        top = jnp.max(s, axis=1, keepdims=True)
        peak = top if peak is None else jnp.maximum(peak, top)
    total, out = None, None
    for s, v in zip(parts, values):
        w = jnp.exp2((s - peak) * LOG2)
        part = jnp.sum(w, axis=1, keepdims=True)
        prod = jnp.dot(w.astype(jnp.bfloat16), v, preferred_element_type=jnp.float32)
        total = part if total is None else total + part
        out = prod if out is None else out + prod
    return peak, total, out


def make_kernel(side, nt, heads):
    ctx_count = side * side

    def kernel(
        len_ref, span_q_hbm, span_kv_hbm, cache_hbm, anchor_hbm, queries_hbm, weight_hbm,
        span_out_hbm, answer_hbm,
        span_q, span_kv, cache, anchor, queries, weight, q_rows, bias,
        q_all, anc, ro_send, rl_send, ro, rl, co, cl, att, att_f, proj, tpr, out, ans,
        in_sem, ss, rs, out_sem,
    ):
        rows = q_all.shape[1] * q_all.shape[2]
        ctx = lax.axis_index("ctx")
        t = lax.axis_index("tp")
        par = lax.rem(t, 2)
        lo, hi = lax.rem(ctx, side), lax.div(ctx, side)
        a = lo + par * (hi - lo)
        b = hi + par * (lo - hi)

        def at(pa, pb):
            first = pb * side + pa
            return {"ctx": first + par * (pa * side + pb - first)}

        def on_a(k):
            return at(lax.rem(a + k, side), b)

        def on_b(k):
            return at(a, lax.rem(b + k, side))

        def on_t(k):
            return {"tp": lax.rem(t + k, nt)}

        def rcopy(src, dst, x, k, dev):
            return pltpu.make_async_remote_copy(
                src_ref=src, dst_ref=dst, send_sem=ss.at[x, k], recv_sem=rs.at[x, k],
                device_id=dev, device_id_type=MESH,
            )

        loads = [
            pltpu.make_async_copy(src, dst, in_sem.at[i])
            for i, (src, dst) in enumerate(
                (
                    (queries_hbm, queries), (anchor_hbm, anchor), (cache_hbm, cache),
                    (span_kv_hbm, span_kv), (span_q_hbm, span_q), (weight_hbm, weight),
                )
            )
        ]
        for load in loads:
            load.start()
        barrier = pltpu.get_barrier_semaphore()
        for k in range(1, side):
            pl.semaphore_signal(barrier, inc=1, device_id=on_a(k), device_id_type=MESH)
            pl.semaphore_signal(barrier, inc=1, device_id=on_b(k), device_id_type=MESH)
        for k in range(1, nt):
            pl.semaphore_signal(barrier, inc=1, device_id=on_t(k), device_id_type=MESH)

        loads[0].wait()
        loads[1].wait()
        wide = queries[...].astype(jnp.float32)
        for i in range(queries.shape[0]):
            for h in range(heads):
                q_rows[i * heads + h : i * heads + h + 1, :] = wide[i : i + 1, h * HD : (h + 1) * HD]
        q_all[b, a] = q_rows[...].astype(jnp.bfloat16)
        own_rows = anchor.shape[1]
        anc[a, :, pl.ds(b * own_rows, own_rows), :] = anchor[...]
        length = len_ref[0]
        column = lax.broadcasted_iota(jnp.int32, bias.shape, 1)
        bias[...] = jnp.where(column < length, 0.0, NEG)

        pl.semaphore_wait(barrier, 2 * (side - 1) + nt - 1)

        far_first = sorted(range(1, side), key=lambda k: -min(k, side - k))

        def qa(k, owner):
            return rcopy(q_all.at[b, owner], q_all.at[b, owner], QA, k, on_a(k))

        def qb(k, owner):
            return rcopy(q_all.at[owner], q_all.at[owner], QB, k, on_b(k))

        def ab(k, owner):
            place = anc.at[a, :, pl.ds(owner * own_rows, own_rows), :]
            return rcopy(place, place, AB, k, on_b(k))

        def aa(k, owner):
            return rcopy(anc.at[owner], anc.at[owner], AA, k, on_a(k))

        for k in far_first:
            qa(k, a).start()
        for k in far_first:
            ab(k, b).start()
        for load in loads[2:]:
            load.wait()
        for k in far_first:
            qa(k, lax.rem(a + side - k, side)).wait_recv()
        for k in far_first:
            qb(k, b).start()
        for k in far_first:
            ab(k, lax.rem(b + side - k, side)).wait_recv()
        for k in far_first:
            aa(k, a).start()

        diag = lax.broadcasted_iota(jnp.int32, (rows, rows), 0) == lax.broadcasted_iota(
            jnp.int32, (rows, rows), 1
        )

        def as_row(col):
            return jnp.sum(jnp.where(diag, col, 0.0), axis=0, keepdims=True)

        def as_col(row):
            return jnp.sum(jnp.where(diag, row, 0.0), axis=1, keepdims=True)

        def query_block(owner, o_ref, l_ref):
            q = q_all[owner].reshape(rows, HD)
            parts = [
                scores(q, cache[0]) + bias[0:1, :],
                scores(q, span_kv[0]),
                scores(q, anchor[0]),
            ]
            peak, total, o = softmax_parts(parts, [cache[1], span_kv[1], anchor[1]])
            o_ref[...] = (o / total).astype(jnp.bfloat16)
            lse = as_row(peak * LOG2 + jnp.log2(total))
            l_ref[...] = jnp.broadcast_to(lse, l_ref.shape)

        query_block(b, ro.at[b], rl.at[b])

        def ro_copy(k, src, owner):
            return rcopy(src, ro.at[owner], RO, k, on_b(k))

        def rl_copy(k, src, owner):
            return rcopy(src, rl.at[owner], RL, k, on_b(k))

        def one_block(i, carry):
            k = lax.rem(i, 2) * lax.div(i + 1, 2) + (1 - lax.rem(i, 2)) * (side - lax.div(i, 2))
            owner = lax.rem(b + side - k, side)
            qb(k, owner).wait_recv()
            query_block(owner, ro_send.at[owner], rl_send.at[owner])
            back = side - k
            ro_copy(back, ro_send.at[owner], b).start()
            rl_copy(back, rl_send.at[owner], b).start()
            return carry

        lax.fori_loop(1, side, one_block, 0)

        def combine(o_ref, l_ref):
            lse = [l_ref[i, 0:1, :] for i in range(side)]
            peak = lse[0]
            for x in lse[1:]:
                peak = jnp.maximum(peak, x)
            weights = [jnp.exp2(x - peak) for x in lse]
            total = weights[0]
            for w in weights[1:]:
                total = total + w
            o = None
            for i in range(side):
                term = as_col(weights[i] / total) * o_ref[i].astype(jnp.float32)
                o = term if o is None else o + term
            return o.astype(jnp.bfloat16), peak + jnp.log2(total)

        for k in range(1, side):
            owner = lax.rem(b + side - k, side)
            ro_copy(k, ro_send.at[owner], owner).wait_recv()
            rl_copy(k, rl_send.at[owner], owner).wait_recv()
        o, lse = combine(ro, rl)
        co[a] = o
        cl[a] = jnp.broadcast_to(lse, cl.shape[1:])

        def co_copy(k, owner):
            return rcopy(co.at[owner], co.at[owner], CO, k, on_a(k))

        def cl_copy(k, owner):
            return rcopy(cl.at[owner], cl.at[owner], CL, k, on_a(k))

        for k in far_first:
            co_copy(k, a).start()
            cl_copy(k, a).start()

        for k in range(1, side):
            aa(k, lax.rem(a + side - k, side)).wait_recv()
        new_rows = span_q.shape[0]
        causal = lax.broadcasted_iota(jnp.int32, (new_rows, new_rows), 1) <= lax.broadcasted_iota(
            jnp.int32, (new_rows, new_rows), 0
        )

        def one_head(h, carry):
            cols = pl.ds(pl.multiple_of(h * HD, HD), HD)
            q = span_q[:, cols]
            anc_k = anc[:, 0].reshape(-1, HD)
            anc_v = anc[:, 1].reshape(-1, HD)
            parts = [
                scores(q, anc_k),
                scores(q, cache[0]) + bias[0:1, :],
                jnp.where(causal, scores(q, span_kv[0]), NEG),
            ]
            _, total, o = softmax_parts(parts, [anc_v, cache[1], span_kv[1]])
            out[:, cols] = (o / total).astype(jnp.bfloat16)
            return carry

        lax.fori_loop(0, heads // 2, one_head, 0)

        for k in range(1, side):
            owner = lax.rem(a + side - k, side)
            co_copy(k, owner).wait_recv()
            cl_copy(k, owner).wait_recv()
        o, _ = combine(co, cl)
        att[b] = o

        def gb(k, owner):
            return rcopy(att.at[owner], att.at[owner], GB, k, on_b(k))

        for k in far_first:
            gb(k, b).start()

        lax.fori_loop(heads // 2, heads, one_head, 0)
        store = pltpu.make_async_copy(out, span_out_hbm, out_sem.at[0])
        store.start()

        for k in range(1, side):
            gb(k, lax.rem(b + side - k, side)).wait_recv()
        att_f[...] = att[...].reshape(-1, HD).astype(jnp.float32)
        count = att_f.shape[0] // heads
        per = count // ctx_count
        row = lax.broadcasted_iota(jnp.int32, (count, count), 0)
        col = lax.broadcasted_iota(jnp.int32, (count, count), 1)
        dev, sub = lax.div(row, per), lax.rem(row, per)
        swapped = (lax.rem(dev, side) * side + lax.div(dev, side)) * per + sub
        source = row + par * (swapped - row)
        perm = jnp.where(col == source, 1.0, 0.0).astype(jnp.bfloat16)
        total = None
        for h in range(heads):
            rows_h = att_f[pl.ds(h, count, stride=heads), :].astype(jnp.bfloat16)
            rows_h = jnp.dot(perm, rows_h, preferred_element_type=jnp.float32)
            term = jnp.dot(
                rows_h.astype(jnp.bfloat16), weight[h * HD : (h + 1) * HD, :],
                preferred_element_type=jnp.float32,
            )
            total = term if total is None else total + term
        proj[...] = total.reshape(proj.shape)
        tpr[t] = proj[t]

        def tp_copy(k, piece, owner):
            return rcopy(proj.at[piece], tpr.at[owner], TP, k, on_t(k))

        for k in range(1, nt):
            tp_copy(k, lax.rem(t + k, nt), t).start()
        for k in range(1, nt):
            owner = lax.rem(t + nt - k, nt)
            tp_copy(k, owner, owner).wait_recv()
        total = tpr[0]
        for i in range(1, nt):
            total = total + tpr[i]
        ans[...] = total.astype(jnp.bfloat16)
        final = pltpu.make_async_copy(ans, answer_hbm, out_sem.at[1])
        final.start()

        for k in range(1, side):
            peer = lax.rem(b + k, side)
            qa(k, a).wait_send()
            qb(k, b).wait_send()
            ab(k, b).wait_send()
            aa(k, a).wait_send()
            ro_copy(k, ro_send.at[peer], b).wait_send()
            rl_copy(k, rl_send.at[peer], b).wait_send()
            co_copy(k, a).wait_send()
            cl_copy(k, a).wait_send()
            gb(k, b).wait_send()
        for k in range(1, nt):
            tp_copy(k, lax.rem(t + k, nt), t).wait_send()
        store.wait()
        final.wait()

    return kernel


def make_local(ctx_count, nt):
    side = math.isqrt(ctx_count)

    def local(span_q, span_kv, cache_kv, anchor_kv, block_len, queries, out_weight):
        heads = span_q.shape[1] // HD
        per = queries.shape[0]
        chunk = per * heads
        rows = side * chunk
        own = anchor_kv.shape[1]
        cols = out_weight.shape[1]
        answer_rows = per * ctx_count // nt
        any_spec = pl.BlockSpec(memory_space=pl.ANY)
        bf16, f32 = jnp.bfloat16, jnp.float32
        vmem = pltpu.VMEM
        return pl.pallas_call(
            make_kernel(side, nt, heads),
            name="star",
            out_shape=(
                jax.ShapeDtypeStruct(span_q.shape, bf16),
                jax.ShapeDtypeStruct((answer_rows, cols), bf16),
            ),
            in_specs=[pl.BlockSpec(memory_space=pltpu.SMEM)] + [any_spec] * 6,
            out_specs=(any_spec, any_spec),
            scratch_shapes=[
                vmem(span_q.shape, bf16),
                vmem(span_kv.shape, bf16),
                vmem(cache_kv.shape, bf16),
                vmem(anchor_kv.shape, bf16),
                vmem(queries.shape, bf16),
                vmem(out_weight.shape, bf16),
                vmem((chunk, HD), f32),
                vmem((8, cache_kv.shape[1]), f32),
                vmem((side, side, chunk, HD), bf16),
                vmem((side, 2, side * own, HD), bf16),
                vmem((side, rows, HD), bf16),
                vmem((side, 8, rows), f32),
                vmem((side, rows, HD), bf16),
                vmem((side, 8, rows), f32),
                vmem((side, rows, HD), bf16),
                vmem((side, 8, rows), f32),
                vmem((side, rows, HD), bf16),
                vmem((side * rows, HD), f32),
                vmem((nt, answer_rows, cols), f32),
                vmem((nt, answer_rows, cols), f32),
                vmem(span_q.shape, bf16),
                vmem((answer_rows, cols), bf16),
                pltpu.SemaphoreType.DMA((6,)),
                pltpu.SemaphoreType.DMA((10, 8)),
                pltpu.SemaphoreType.DMA((10, 8)),
                pltpu.SemaphoreType.DMA((2,)),
            ],
            compiler_params=pltpu.CompilerParams(collective_id=0, has_side_effects=True),
        )(block_len, span_q, span_kv, cache_kv, anchor_kv, queries, out_weight)

    return local


def solution(mesh):
    placed = (
        P("ctx", "tp"),
        P(None, "ctx", "tp"),
        P(None, "ctx", "tp"),
        P(None, "ctx", "tp"),
        P("ctx"),
        P("ctx", "tp"),
        P("tp", "ctx"),
    )
    return jax.shard_map(
        make_local(mesh.shape["ctx"], mesh.shape["tp"]),
        mesh=mesh,
        in_specs=placed,
        out_specs=(P("ctx", "tp"), P("tp", "ctx")),
        check_vma=False,
    )
```

time: 454 us -> 66.6 us (0.15)
  blocking collectives: 269 us -> 0 us
  waiting for transfers between devices: 125 us -> 0 us
  Pallas kernels: 0 us -> 62.9 us
  matrix products: 23.1 us -> 0 us
  other arithmetic: 13.6 us -> 0 us
  between operations: 14.6 us -> 1.29 us
    pmax x1 -> x0, blocking collectives: 114 us -> none  [local(): global_max = lax.pmax(part_max, 'ctx')]
    psum x1 -> x0, blocking collectives: 110 us -> none  [local(): lax.psum((part_sum * rescale, part_values * jnp.repeat(rescale, HD, axis=...]
    pallas_call x0 -> x1, Pallas kernels: none -> 62.9 us  [local(): pl.pallas_call(make_kernel(side, nt, heads), name='star', out_shape=(jax....]
    psum x1 -> x0, waiting for transfers between devices: 49 us -> none  [local(): lax.psum((part_sum * rescale, part_values * jnp.repeat(rescale, HD, axis=...]
    all_gather x1 -> x0, blocking collectives: 45.7 us -> none  [local(): query_all = lax.all_gather(queries, 'ctx', axis=0, tiled=True)]
    reduce_scatter x1 -> x0, waiting for transfers between devices: 39.6 us -> none  [local(): lax.psum_scatter(partial_value, 'tp', scatter_dimension=0, tiled=True)]
    all_gather x1 -> x0, waiting for transfers between devices: 35.5 us -> none  [local(): anchor_all = lax.all_gather(anchor_kv, 'ctx', axis=1, tiled=True)]
    dot_general x33 -> x0, matrix products: 23.1 us -> none  [the longest x16 15.1 us: per_head(): jnp.einsum('qd,nd->qn', q_head, key_rows, preferred_element_type=jnp.floa...]
  transfers between devices with their start and end apart: 3 -> 0, of which waited for: 3 -> 0; matrix products, arithmetic and copies ran while one was open for 5% -> 0% of each run, Pallas kernels for 0% -> 0%
where the time goes in v1:
time: 66.6 us; the launch traced here: 66.4 us
  Pallas kernels  62.9 us (94%)
  local copies, waits for them, and re-layouts  2.27 us (3%)
  between operations  1.29 us (2%)
    pallas_call x1, Pallas kernels, local(): pl.pallas_call(make_kernel(side, nt, heads), name='star', out_shape=(jax....  62.9 us
    unnamed x4, local copies, waits for them, and re-layouts  2.27 us

profile of v1, /device:TPU:1, one launch (start us, length us, event | category | flops | bytes accessed | tf_op | source)
XLA Modules:
  0.0 66.4 jit_solution(2170328572690918875)
XLA Ops:
  1.3 62.9 %star.1 = (bf16[128,1024]{1,0:T(8,128)(2,1)}, bf16[16,128]{1,0:T(8,128)(2,1)}) custom-call(s32[1]{0:T(128)S(6)} %copy.11.len_ref, bf16[128,1024]{1,0:T(8,128)(2,1)} %span_q_hbm.1, bf16[2,128,128]{2,1,0:T(8,128)(2,1)} %span_kv_hbm.1, bf16[2,1024,128]{2,1,0:T(8,128)(2,1)} %cache_hbm.1, bf16[2,32,128]{2,1,0:T(8,128)(2,1)} %anchor_hbm.1, ...), custom_call_target="tpu_custom_call" | custom-call | tf_op jit(solution)/shard_map/star/pallas_call | solution.py:323
  64.2 0.0 copy-start
  64.2 1.7 %copy.12 = bf16[128,1024]{1,0:T(8,128)(2,1)} copy(bf16[128,1024]{1,0:T(8,128)(2,1)} %get-tuple-element.4) | data formatting | bytes 524288
  65.8 0.0 copy-done
  65.8 0.6 copy.13
Async XLA Ops:
  64.2 1.7 %copy-start = (bf16[16,128]{1,0:T(8,128)(2,1)S(1)}, bf16[16,128]{1,0:T(8,128)(2,1)}, u32[]{:S(2)}) copy-start(bf16[16,128]{1,0:T(8,128)(2,1)} %get-tuple-element.5) | copy-start | bytes 12292

commit v2 on v1

v2 whole, which is shorter than its diff:
```python
import math

import jax
import jax.numpy as jnp
from jax import lax
from jax.experimental import pallas as pl
from jax.experimental.pallas import tpu as pltpu
from jax.sharding import PartitionSpec as P

HD = 128
NEG = -1e30
MESH = pl.DeviceIdType.MESH
LOG2 = math.log2(math.e) / math.sqrt(HD)

QA, QB, AB, AA, RO, RL, CO, CL, GB, TP = range(10)


def scores(q, k):
    return lax.dot_general(q, k, (((1,), (1,)), ((), ())), preferred_element_type=jnp.float32)


def softmax_parts(parts, values):
    peak = None
    for s in parts:
        top = jnp.max(s, axis=1, keepdims=True)
        peak = top if peak is None else jnp.maximum(peak, top)
    total, out = None, None
    for s, v in zip(parts, values):
        w = jnp.exp2((s - peak) * LOG2)
        part = jnp.sum(w, axis=1, keepdims=True)
        prod = jnp.dot(w.astype(jnp.bfloat16), v, preferred_element_type=jnp.float32)
        total = part if total is None else total + part
        out = prod if out is None else out + prod
    return peak, total, out


def wide(x, columns):
    return x if columns == x.shape[1] else jnp.concatenate([x] * (columns // x.shape[1]), axis=1)


def lane_softmax(parts, values, before=None):
    top = None
    for s in parts:
        for c in range(0, s.shape[1], HD):
            piece = s[:, c : c + HD]
            top = piece if top is None else jnp.maximum(top, piece)
    peak = jnp.broadcast_to(jnp.max(top, axis=1, keepdims=True), top.shape)
    if before is not None:
        peak = jnp.maximum(peak, before)
    total, out = None, None
    for s, v in zip(parts, values):
        w = jnp.exp2((s - wide(peak, s.shape[1])) * LOG2)
        for c in range(0, w.shape[1], HD):
            piece = w[:, c : c + HD]
            total = piece if total is None else total + piece
        prod = jnp.dot(w.astype(jnp.bfloat16), v, preferred_element_type=jnp.float32)
        out = prod if out is None else out + prod
    return peak, total, out


def make_kernel(side, nt, heads):
    ctx_count = side * side
    half = side // 2

    def kernel(
        len_hbm, span_q_hbm, span_kv_hbm, cache_hbm, anchor_hbm, queries_hbm, weight_hbm,
        out, ans,
        len_ref, span_q, span_kv, cache, anchor, queries, weight, q_rows, bias,
        mine, qx, q_all, anc, ro_send, rl_send, ro, rl, co, cl, done, att, att_f, proj, tpr,
        f_peak, f_sum, f_out,
        in_sem, ss, rs,
    ):
        rows = q_all.shape[1] * q_all.shape[2]
        ctx = lax.axis_index("ctx")
        t = lax.axis_index("tp")
        par = lax.rem(t, 2)
        lo, hi = lax.rem(ctx, side), lax.div(ctx, side)
        a = lo + par * (hi - lo)
        b = hi + par * (lo - hi)

        other = t + 1 - 2 * par

        def at(pa, pb, core):
            first = pb * side + pa
            return {"ctx": first + par * (pa * side + pb - first), "tp": core}

        def on_a(k):
            return at(lax.rem(a + k, side), b, t)

        def on_b(k):
            return at(a, lax.rem(b + k, side), t)

        def over_a(k):
            return at(lax.rem(a + k, side), b, other)

        def over_b(k):
            return at(a, lax.rem(b + k, side), other)

        def back(x, k):
            return lax.rem(x + side - k, side)

        def on_t(k):
            return {"tp": lax.rem(t + k, nt)}

        def rcopy(src, dst, x, k, dev):
            return pltpu.make_async_remote_copy(
                src_ref=src, dst_ref=dst, send_sem=ss.at[x, k], recv_sem=rs.at[x, k],
                device_id=dev, device_id_type=MESH,
            )

        new_rows = out.shape[0]
        pairs = [
            (queries_hbm, queries), (anchor_hbm, anchor), (len_hbm, len_ref), (cache_hbm, cache),
            (span_kv_hbm, span_kv), (weight_hbm, weight),
        ]
        for h in range(heads):
            pairs.append(
                (span_q_hbm.at[:, h * HD : (h + 1) * HD], span_q.at[h * new_rows : (h + 1) * new_rows])
            )
        loads = [
            pltpu.make_async_copy(src, dst, in_sem.at[i]) for i, (src, dst) in enumerate(pairs)
        ]
        barrier = pltpu.get_barrier_semaphore()
        for k in range(1, side):
            for peer in (on_a(k), on_b(k), over_a(k), over_b(k)):
                pl.semaphore_signal(barrier, inc=1, device_id=peer, device_id_type=MESH)
        for k in range(1, nt):
            pl.semaphore_signal(barrier, inc=1, device_id=on_t(k), device_id_type=MESH)

        for load in loads:
            load.start()

        loads[0].wait()
        loads[1].wait()
        wide = queries[...].astype(jnp.float32)
        for i in range(queries.shape[0]):
            for h in range(heads):
                q_rows[i * heads + h : i * heads + h + 1, :] = wide[i : i + 1, h * HD : (h + 1) * HD]
        mine[...] = q_rows[...].astype(jnp.bfloat16)
        own_rows = anchor.shape[1]
        anc[b, :, pl.ds(a * own_rows, own_rows), :] = anchor[...]
        loads[2].wait()
        length = len_ref[0]
        column = lax.broadcasted_iota(jnp.int32, bias.shape, 1)
        bias[...] = jnp.where(column < length, 0.0, NEG)

        pl.semaphore_wait(barrier, 4 * (side - 1) + nt - 1)

        far_first = sorted(range(1, side), key=lambda k: -min(k, side - k))
        far_all = far_first + [0]

        def qa(k, owner):
            return rcopy(mine, qx.at[owner], QA, k, over_a(k))

        def qb_chunk(k, chunk):
            return rcopy(qx.at[chunk], q_all.at[a, chunk], QB, k, over_a(k))

        def qb(k, owner):
            return rcopy(qx, q_all.at[owner], QB, k, over_a(k))

        def ab(k, owner):
            place = anc.at[b, :, pl.ds(owner * own_rows, own_rows), :]
            return rcopy(place, place, AB, k, on_a(k))

        def right(step, slot):
            return rcopy(anc.at[slot], anc.at[slot], AA, step - 1, on_b(1))

        def left(step, slot):
            return rcopy(anc.at[slot], anc.at[slot], AA, half + step - 1, on_b(side - 1))

        def slot_at(offset):
            return lax.rem(b + side + offset, side)

        def ring_send(step):
            if step <= half:
                right(step, slot_at(1 - step)).start()
            if step <= half - 1:
                left(step, slot_at(step - 1)).start()

        def ring_recv(step):
            got = []
            if step <= half:
                got.append(slot_at(-step))
                right(step, got[-1]).wait_recv()
            if step <= half - 1:
                got.append(slot_at(step))
                left(step, got[-1]).wait_recv()
            return got

        for k in far_all:
            qa(k, a).start()
        for k in far_first:
            ab(k, a).start()

        group = min(heads, 4) * new_rows
        tri_row = lax.rem(lax.broadcasted_iota(jnp.int32, (group, new_rows), 0), new_rows)
        tri_col = lax.broadcasted_iota(jnp.int32, (group, new_rows), 1)

        def first_local(i, carry):
            r = pl.ds(pl.multiple_of(i * group, group), group)
            q = span_q[r, :]
            parts = [
                scores(q, cache[0]) + bias[0:1, :],
                jnp.where(tri_col <= tri_row, scores(q, span_kv[0]), NEG),
            ]
            peak, total, o = lane_softmax(parts, [cache[1], span_kv[1]])
            f_peak[r, :] = peak
            f_sum[r, :] = total
            f_out[r, :] = o
            return carry

        def first_anchor(slots, last=False):
            def body(i, carry):
                r = pl.ds(pl.multiple_of(i * group, group), group)
                q = span_q[r, :]
                parts = [scores(q, anc[s, 0]) for s in slots]
                before = f_peak[r, :]
                peak, total, o = lane_softmax(parts, [anc[s, 1] for s in slots], before)
                shrink = jnp.exp2((before - peak) * LOG2)
                total = f_sum[r, :] * shrink + total
                o = f_out[r, :] * shrink + o
                if last:
                    f_out[r, :] = o / jnp.sum(total, axis=1, keepdims=True)
                else:
                    f_peak[r, :] = peak
                    f_sum[r, :] = total
                    f_out[r, :] = o
                return carry

            lax.fori_loop(0, heads * new_rows // group, body, 0)

        for load in loads[3:]:
            load.wait()
        def forward(offsets):
            for d in offsets:
                chunk = back(b, d)
                qa(d, chunk).wait_recv()
                for k in far_all:
                    qb_chunk(k, chunk).start()

        groups = heads * new_rows // group
        lax.fori_loop(0, (groups + 1) // 2, first_local, 0)
        forward([0] + sorted({1, side - 1}))
        lax.fori_loop((groups + 1) // 2, groups, first_local, 0)
        for d in range(2, half + 1):
            forward(sorted({d, side - d}))
        for k in far_first:
            ab(k, back(a, k)).wait_recv()
        ring_send(1)

        diag = lax.broadcasted_iota(jnp.int32, (rows, rows), 0) == lax.broadcasted_iota(
            jnp.int32, (rows, rows), 1
        )

        def as_row(col):
            return jnp.sum(jnp.where(diag, col, 0.0), axis=0, keepdims=True)

        def as_col(row):
            return jnp.sum(jnp.where(diag, row, 0.0), axis=1, keepdims=True)

        def query_block(owner, o_ref, l_ref):
            q = q_all[owner].reshape(rows, HD)
            parts = [
                scores(q, cache[0]) + bias[0:1, :],
                scores(q, span_kv[0]),
                scores(q, anchor[0]),
            ]
            peak, total, o = softmax_parts(parts, [cache[1], span_kv[1], anchor[1]])
            o_ref[...] = (o / total).astype(jnp.bfloat16)
            l_ref[...] = as_row(peak * LOG2 + jnp.log2(total))

        def ro_copy(k, block, owner):
            return rcopy(ro_send.at[block], ro.at[owner], RO, k, over_b(k))

        def rl_copy(k, block, owner):
            return rcopy(rl_send.at[block], rl.at[owner], RL, k, over_b(k))

        def some_blocks(offsets):
            owners = [back(b, k) for k in offsets]
            for k, owner in zip(offsets, owners):
                qb(k, owner).wait_recv()
            for owner in owners:
                query_block(owner, ro_send.at[owner], rl_send.at[owner])
            for k, owner in zip(offsets, owners):
                k = lax.rem(side - k, side)
                ro_copy(k, owner, b).start()
                rl_copy(k, owner, b).start()

        some_blocks([0])


        def two_blocks(i, carry):
            some_blocks([i, side - i])
            return carry

        lax.fori_loop(1, half, two_blocks, 0)
        some_blocks([half])

        slots = [b] + ring_recv(1)
        ring_send(2)
        first_anchor(slots, last=half == 1)

        def combine(o_ref, l_ref):
            lse = [l_ref[i] for i in range(side)]
            peak = lse[0]
            for x in lse[1:]:
                peak = jnp.maximum(peak, x)
            weights = [jnp.exp2(x - peak) for x in lse]
            total = weights[0]
            for w in weights[1:]:
                total = total + w
            o = None
            for i in range(side):
                term = as_col(weights[i] / total) * o_ref[i].astype(jnp.float32)
                o = term if o is None else o + term
            return o.astype(jnp.bfloat16), peak + jnp.log2(total)

        for k in range(side):
            ro_copy(k, 0, back(a, k)).wait_recv()
            rl_copy(k, 0, back(a, k)).wait_recv()
        o, lse = combine(ro, rl)
        co[b] = o
        cl[b] = lse

        def co_copy(k, owner):
            return rcopy(co.at[owner], co.at[owner], CO, k, on_b(k))

        def cl_copy(k, owner):
            return rcopy(cl.at[owner], cl.at[owner], CL, k, on_b(k))

        for k in far_first:
            co_copy(k, b).start()
            cl_copy(k, b).start()

        if half > 1:
            slots = ring_recv(2)
            ring_send(3)
            first_anchor(slots, last=half == 2)
        for k in range(1, side):
            co_copy(k, back(b, k)).wait_recv()
            cl_copy(k, back(b, k)).wait_recv()
        o, _ = combine(co, cl)
        done[...] = o

        def gb(k, owner):
            return rcopy(done, att.at[owner], GB, k, over_a(k))

        for k in far_all:
            gb(k, a).start()

        for step in range(3, half):
            slots = ring_recv(step)
            ring_send(step + 1)
            first_anchor(slots)

        for k in range(side):
            gb(k, back(b, k)).wait_recv()
        att_f[...] = att[...].reshape(-1, HD).astype(jnp.float32)
        count = att_f.shape[0] // heads
        per = count // ctx_count
        row = lax.broadcasted_iota(jnp.int32, (count, count), 0)
        col = lax.broadcasted_iota(jnp.int32, (count, count), 1)
        dev, sub = lax.div(row, per), lax.rem(row, per)
        swapped = (lax.rem(dev, side) * side + lax.div(dev, side)) * per + sub
        source = row + par * (swapped - row)
        perm = jnp.where(col == source, 1.0, 0.0).astype(jnp.bfloat16)
        total = None
        for h in range(heads):
            rows_h = att_f[pl.ds(h, count, stride=heads), :].astype(jnp.bfloat16)
            rows_h = jnp.dot(perm, rows_h, preferred_element_type=jnp.float32)
            term = jnp.dot(
                rows_h.astype(jnp.bfloat16), weight[h * HD : (h + 1) * HD, :],
                preferred_element_type=jnp.float32,
            )
            total = term if total is None else total + term
        proj[...] = total.reshape(proj.shape)
        tpr[t] = proj[t]

        def tp_copy(k, piece, owner):
            return rcopy(proj.at[piece], tpr.at[owner], TP, k, on_t(k))

        for k in range(1, nt):
            tp_copy(k, lax.rem(t + k, nt), t).start()

        if half > 2:
            slots = ring_recv(half)
            first_anchor(slots, last=True)
        for h in range(heads):
            out[:, h * HD : (h + 1) * HD] = f_out[h * new_rows : (h + 1) * new_rows, :].astype(jnp.bfloat16)

        for k in range(1, nt):
            owner = lax.rem(t + nt - k, nt)
            tp_copy(k, owner, owner).wait_recv()
        total = tpr[0]
        for i in range(1, nt):
            total = total + tpr[i]
        ans[...] = total.astype(jnp.bfloat16)

        for step in range(1, half + 1):
            right(step, slot_at(1 - step)).wait_send()
            if step < half:
                left(step, slot_at(step - 1)).wait_send()
        for k in range(side):
            qa(k, a).wait_send()
            qb(k, a).wait_send()
            ro_copy(k, 0, b).wait_send()
            rl_copy(k, 0, b).wait_send()
            gb(k, a).wait_send()
        for k in range(1, side):
            ab(k, a).wait_send()
            co_copy(k, b).wait_send()
            cl_copy(k, b).wait_send()
        for k in range(1, nt):
            tp_copy(k, lax.rem(t + k, nt), t).wait_send()

    return kernel


def make_local(ctx_count, nt):
    side = math.isqrt(ctx_count)

    def local(span_q, span_kv, cache_kv, anchor_kv, block_len, queries, out_weight):
        new_rows = span_q.shape[0]
        heads = span_q.shape[1] // HD
        per = queries.shape[0]
        chunk = per * heads
        rows = side * chunk
        own = anchor_kv.shape[1]
        cols = out_weight.shape[1]
        answer_rows = per * ctx_count // nt
        any_spec = pl.BlockSpec(memory_space=pl.ANY)
        vmem_spec = pl.BlockSpec(memory_space=pltpu.VMEM)
        bf16, f32 = jnp.bfloat16, jnp.float32
        vmem = pltpu.VMEM
        return pl.pallas_call(
            make_kernel(side, nt, heads),
            name="star",
            out_shape=(vmem(span_q.shape, bf16), vmem((answer_rows, cols), bf16)),
            in_specs=[any_spec] * 7,
            out_specs=(vmem_spec, vmem_spec),
            scratch_shapes=[
                pltpu.SMEM(block_len.shape, jnp.int32),
                vmem((heads * new_rows, HD), bf16),
                vmem(span_kv.shape, bf16),
                vmem(cache_kv.shape, bf16),
                vmem(anchor_kv.shape, bf16),
                vmem(queries.shape, bf16),
                vmem(out_weight.shape, bf16),
                vmem((chunk, HD), f32),
                vmem((8, cache_kv.shape[1]), f32),
                vmem((chunk, HD), bf16),
                vmem((side, chunk, HD), bf16),
                vmem((side, side, chunk, HD), bf16),
                vmem((side, 2, side * own, HD), bf16),
                vmem((side, rows, HD), bf16),
                vmem((side, 1, rows), f32),
                vmem((side, rows, HD), bf16),
                vmem((side, 1, rows), f32),
                vmem((side, rows, HD), bf16),
                vmem((side, 1, rows), f32),
                vmem((rows, HD), bf16),
                vmem((side, rows, HD), bf16),
                vmem((side * rows, HD), f32),
                vmem((nt, answer_rows, cols), f32),
                vmem((nt, answer_rows, cols), f32),
                vmem((heads * new_rows, HD), f32),
                vmem((heads * new_rows, HD), f32),
                vmem((heads * new_rows, HD), f32),
                pltpu.SemaphoreType.DMA((6 + heads,)),
                pltpu.SemaphoreType.DMA((10, 8)),
                pltpu.SemaphoreType.DMA((10, 8)),
            ],
            compiler_params=pltpu.CompilerParams(collective_id=0, has_side_effects=True),
        )(block_len, span_q, span_kv, cache_kv, anchor_kv, queries, out_weight)

    return local


def solution(mesh):
    placed = (
        P("ctx", "tp"),
        P(None, "ctx", "tp"),
        P(None, "ctx", "tp"),
        P(None, "ctx", "tp"),
        P("ctx"),
        P("ctx", "tp"),
        P("tp", "ctx"),
    )
    return jax.shard_map(
        make_local(mesh.shape["ctx"], mesh.shape["tp"]),
        mesh=mesh,
        in_specs=placed,
        out_specs=(P("ctx", "tp"), P("tp", "ctx")),
        check_vma=False,
    )
```

time: 66.6 us -> 54.9 us (0.82)
  Pallas kernels: 62.9 us -> 52.2 us
  local copies, waits for them, and re-layouts: 2.27 us -> 1.3 us
    pallas_call x1, Pallas kernels: 62.9 us -> 52.2 us  [local(): pl.pallas_call(make_kernel(side, nt, heads), name='star', out_shape=(vmem...]
    unnamed x4 -> x2, local copies, waits for them, and re-layouts: 2.27 us -> 1.3 us
where the time goes in v2:
time: 54.9 us; the launch traced here: 54.8 us
  Pallas kernels  52.2 us (95%)
  local copies, waits for them, and re-layouts  1.3 us (2%)
  between operations  1.29 us (2%)
    pallas_call x1, Pallas kernels, local(): pl.pallas_call(make_kernel(side, nt, heads), name='star', out_shape=(vmem...  52.2 us
    unnamed x2, local copies, waits for them, and re-layouts  1.3 us

profile of v2, /device:TPU:1, one launch (start us, length us, event | category | flops | bytes accessed | tf_op | source)
XLA Modules:
  0.0 54.8 jit_solution(1055766385660487224)
XLA Ops:
  1.3 52.2 %star.1 = (bf16[128,1024]{1,0:T(8,128)(2,1)S(1)}, bf16[16,128]{1,0:T(8,128)(2,1)S(1)}) custom-call(s32[1]{0:T(128)S(6)} %copy.13.len_hbm, bf16[128,1024]{1,0:T(8,128)(2,1)} %span_q_hbm.1, bf16[2,128,128]{2,1,0:T(8,128)(2,1)} %span_kv_hbm.1, bf16[2,1024,128]{2,1,0:T(8,128)(2,1)} %cache_hbm.1, bf16[2,32,128]{2,1,0:T(8,128)(2,1)} %anchor_hbm.1, ...), custom_call_target="tpu_custom_call" | custom-call | tf_op jit(solution)/shard_map/star/pallas_call | solution.py:435
  53.5 0.7 %copy.11 = bf16[128,1024]{1,0:T(8,128)(2,1)} copy(bf16[128,1024]{1,0:T(8,128)(2,1)S(1)} %get-tuple-element.2) | data formatting | bytes 524288
  54.2 0.6 %copy.12 = bf16[16,128]{1,0:T(8,128)(2,1)} copy(bf16[16,128]{1,0:T(8,128)(2,1)S(1)} %get-tuple-element.3) | data formatting | bytes 8192

commit v3 on v2

--- a/solution.py
+++ b/solution.py
@@ -12,7 +12,7 @@
 MESH = pl.DeviceIdType.MESH
 LOG2 = math.log2(math.e) / math.sqrt(HD)
 
-QA, QB, AB, AA, RO, RL, CO, CL, GB, TP = range(10)
+SENDS = QA, QB, AB, AA, RO, RL, CO, CL, GB, TP = range(10)
 
 
 def scores(q, k):
@@ -64,11 +64,11 @@
 
     def kernel(
         len_hbm, span_q_hbm, span_kv_hbm, cache_hbm, anchor_hbm, queries_hbm, weight_hbm,
-        out, ans,
+        out_any, ans_any,
         len_ref, span_q, span_kv, cache, anchor, queries, weight, q_rows, bias,
         mine, qx, q_all, anc, ro_send, rl_send, ro, rl, co, cl, done, att, att_f, proj, tpr,
-        f_peak, f_sum, f_out,
-        in_sem, ss, rs,
+        f_peak, f_sum, f_out, out, ans,
+        in_sem, ss, rs, out_sem,
     ):
         rows = q_all.shape[1] * q_all.shape[2]
         ctx = lax.axis_index("ctx")
@@ -102,9 +102,15 @@
         def on_t(k):
             return {"tp": lax.rem(t + k, nt)}
 
+        single = (QA, QB, AA)
+        first_recv, used = {}, 0
+        for x in SENDS:
+            first_recv[x] = used
+            used += side if x in single else 1
+
         def rcopy(src, dst, x, k, dev):
             return pltpu.make_async_remote_copy(
-                src_ref=src, dst_ref=dst, send_sem=ss.at[x, k], recv_sem=rs.at[x, k],
+                src_ref=src, dst_ref=dst, send_sem=ss.at[x], recv_sem=rs.at[first_recv[x] + (k if x in single else 0)],
                 device_id=dev, device_id_type=MESH,
             )
 
@@ -118,7 +124,7 @@
                 (span_q_hbm.at[:, h * HD : (h + 1) * HD], span_q.at[h * new_rows : (h + 1) * new_rows])
             )
         loads = [
-            pltpu.make_async_copy(src, dst, in_sem.at[i]) for i, (src, dst) in enumerate(pairs)
+            pltpu.make_async_copy(src, dst, in_sem.at[min(i, 6)]) for i, (src, dst) in enumerate(pairs)
         ]
         barrier = pltpu.get_barrier_semaphore()
         for k in range(1, side):
@@ -158,6 +164,9 @@
         def qb(k, owner):
             return rcopy(qx, q_all.at[owner], QB, k, over_a(k))
 
+        def all_of(x, ref):
+            return rcopy(ref, ref, x, 0, over_a(0))
+
         def ab(k, owner):
             place = anc.at[b, :, pl.ds(owner * own_rows, own_rows), :]
             return rcopy(place, place, AB, k, on_a(k))
@@ -189,8 +198,6 @@
 
         for k in far_all:
             qa(k, a).start()
-        for k in far_first:
-            ab(k, a).start()
 
         group = min(heads, 4) * new_rows
         tri_row = lax.rem(lax.broadcasted_iota(jnp.int32, (group, new_rows), 0), new_rows)
@@ -229,8 +236,9 @@
 
             lax.fori_loop(0, heads * new_rows // group, body, 0)
 
-        for load in loads[3:]:
+        for load in loads[3:6]:
             load.wait()
+        pltpu.make_async_copy(span_q, span_q, in_sem.at[6]).wait()
         def forward(offsets):
             for d in offsets:
                 chunk = back(b, d)
@@ -240,14 +248,11 @@
 
         groups = heads * new_rows // group
         lax.fori_loop(0, (groups + 1) // 2, first_local, 0)
+        for k in far_first:
+            ab(k, a).start()
         forward([0] + sorted({1, side - 1}))
-        lax.fori_loop((groups + 1) // 2, groups, first_local, 0)
         for d in range(2, half + 1):
             forward(sorted({d, side - d}))
-        for k in far_first:
-            ab(k, back(a, k)).wait_recv()
-        ring_send(1)
-
         diag = lax.broadcasted_iota(jnp.int32, (rows, rows), 0) == lax.broadcasted_iota(
             jnp.int32, (rows, rows), 1
         )
@@ -258,16 +263,20 @@
         def as_col(row):
             return jnp.sum(jnp.where(diag, row, 0.0), axis=1, keepdims=True)
 
-        def query_block(owner, o_ref, l_ref):
-            q = q_all[owner].reshape(rows, HD)
+        def query_blocks(owners):
+            q = [q_all[owner].reshape(rows, HD) for owner in owners]
+            q = q[0] if len(q) == 1 else jnp.concatenate(q, axis=0)
             parts = [
                 scores(q, cache[0]) + bias[0:1, :],
                 scores(q, span_kv[0]),
                 scores(q, anchor[0]),
             ]
             peak, total, o = softmax_parts(parts, [cache[1], span_kv[1], anchor[1]])
-            o_ref[...] = (o / total).astype(jnp.bfloat16)
-            l_ref[...] = as_row(peak * LOG2 + jnp.log2(total))
+            o = (o / total).astype(jnp.bfloat16)
+            lse = peak * LOG2 + jnp.log2(total)
+            for i, owner in enumerate(owners):
+                ro_send[owner] = o[i * rows : (i + 1) * rows]
+                rl_send[owner] = as_row(lse[i * rows : (i + 1) * rows])
 
         def ro_copy(k, block, owner):
             return rcopy(ro_send.at[block], ro.at[owner], RO, k, over_b(k))
@@ -279,8 +288,7 @@
             owners = [back(b, k) for k in offsets]
             for k, owner in zip(offsets, owners):
                 qb(k, owner).wait_recv()
-            for owner in owners:
-                query_block(owner, ro_send.at[owner], rl_send.at[owner])
+            query_blocks(owners)
             for k, owner in zip(offsets, owners):
                 k = lax.rem(side - k, side)
                 ro_copy(k, owner, b).start()
@@ -288,6 +296,9 @@
 
         some_blocks([0])
 
+        all_of(AB, anc.at[b, :, pl.ds(0, (side - 1) * own_rows), :]).wait_recv()
+        ring_send(1)
+
 
         def two_blocks(i, carry):
             some_blocks([i, side - i])
@@ -296,9 +307,9 @@
         lax.fori_loop(1, half, two_blocks, 0)
         some_blocks([half])
 
+        lax.fori_loop((groups + 1) // 2, groups, first_local, 0)
         slots = [b] + ring_recv(1)
         ring_send(2)
-        first_anchor(slots, last=half == 1)
 
         def combine(o_ref, l_ref):
             lse = [l_ref[i] for i in range(side)]
@@ -315,9 +326,8 @@
                 o = term if o is None else o + term
             return o.astype(jnp.bfloat16), peak + jnp.log2(total)
 
-        for k in range(side):
-            ro_copy(k, 0, back(a, k)).wait_recv()
-            rl_copy(k, 0, back(a, k)).wait_recv()
+        all_of(RO, ro).wait_recv()
+        all_of(RL, rl).wait_recv()
         o, lse = combine(ro, rl)
         co[b] = o
         cl[b] = lse
@@ -333,12 +343,12 @@
             cl_copy(k, b).start()
 
         if half > 1:
-            slots = ring_recv(2)
-            ring_send(3)
-            first_anchor(slots, last=half == 2)
-        for k in range(1, side):
-            co_copy(k, back(b, k)).wait_recv()
-            cl_copy(k, back(b, k)).wait_recv()
+            slots = slots + ring_recv(2)
+        first_anchor(slots, last=half <= 2)
+        ring_send(3)
+
+        all_of(CO, co.at[0 : side - 1]).wait_recv()
+        all_of(CL, cl.at[0 : side - 1]).wait_recv()
         o, _ = combine(co, cl)
         done[...] = o
 
@@ -350,11 +360,10 @@
 
         for step in range(3, half):
             slots = ring_recv(step)
+            first_anchor(slots)
             ring_send(step + 1)
-            first_anchor(slots)
-
-        for k in range(side):
-            gb(k, back(b, k)).wait_recv()
+
+        all_of(GB, att).wait_recv()
         att_f[...] = att[...].reshape(-1, HD).astype(jnp.float32)
         count = att_f.shape[0] // heads
         per = count // ctx_count
@@ -387,31 +396,25 @@
             first_anchor(slots, last=True)
         for h in range(heads):
             out[:, h * HD : (h + 1) * HD] = f_out[h * new_rows : (h + 1) * new_rows, :].astype(jnp.bfloat16)
-
-        for k in range(1, nt):
-            owner = lax.rem(t + nt - k, nt)
-            tp_copy(k, owner, owner).wait_recv()
+        store = pltpu.make_async_copy(out, out_any, out_sem.at[0])
+        store.start()
+
+        all_of(TP, tpr.at[0 : nt - 1]).wait_recv()
         total = tpr[0]
         for i in range(1, nt):
             total = total + tpr[i]
         ans[...] = total.astype(jnp.bfloat16)
-
-        for step in range(1, half + 1):
-            right(step, slot_at(1 - step)).wait_send()
-            if step < half:
-                left(step, slot_at(step - 1)).wait_send()
-        for k in range(side):
-            qa(k, a).wait_send()
-            qb(k, a).wait_send()
-            ro_copy(k, 0, b).wait_send()
-            rl_copy(k, 0, b).wait_send()
-            gb(k, a).wait_send()
-        for k in range(1, side):
-            ab(k, a).wait_send()
-            co_copy(k, b).wait_send()
-            cl_copy(k, b).wait_send()
-        for k in range(1, nt):
-            tp_copy(k, lax.rem(t + k, nt), t).wait_send()
+        final = pltpu.make_async_copy(ans, ans_any, out_sem.at[1])
+        final.start()
+
+        for x, ref in (
+            (QA, qx), (QB, q_all), (AB, anc.at[b, :, pl.ds(0, (side - 1) * own_rows), :]),
+            (AA, anc.at[0 : side - 1]), (RO, ro), (RL, rl), (CO, co.at[0 : side - 1]),
+            (CL, cl.at[0 : side - 1]), (GB, att), (TP, tpr.at[0 : nt - 1]),
+        ):
+            all_of(x, ref).wait_send()
+        store.wait()
+        final.wait()
 
     return kernel
 
@@ -429,15 +432,14 @@
         cols = out_weight.shape[1]
         answer_rows = per * ctx_count // nt
         any_spec = pl.BlockSpec(memory_space=pl.ANY)
-        vmem_spec = pl.BlockSpec(memory_space=pltpu.VMEM)
         bf16, f32 = jnp.bfloat16, jnp.float32
         vmem = pltpu.VMEM
         return pl.pallas_call(
             make_kernel(side, nt, heads),
             name="star",
             out_shape=(vmem(span_q.shape, bf16), vmem((answer_rows, cols), bf16)),
-            in_specs=[any_spec] * 7,
-            out_specs=(vmem_spec, vmem_spec),
+            in_specs=[pl.BlockSpec(memory_space=pltpu.HBM)] + [any_spec] * 6,
+            out_specs=(any_spec, any_spec),
             scratch_shapes=[
                 pltpu.SMEM(block_len.shape, jnp.int32),
                 vmem((heads * new_rows, HD), bf16),
@@ -466,9 +468,12 @@
                 vmem((heads * new_rows, HD), f32),
                 vmem((heads * new_rows, HD), f32),
                 vmem((heads * new_rows, HD), f32),
-                pltpu.SemaphoreType.DMA((6 + heads,)),
-                pltpu.SemaphoreType.DMA((10, 8)),
-                pltpu.SemaphoreType.DMA((10, 8)),
+                vmem(span_q.shape, bf16),
+                vmem((answer_rows, cols), bf16),
+                pltpu.SemaphoreType.DMA((7,)),
+                pltpu.SemaphoreType.DMA((len(SENDS),)),
+                pltpu.SemaphoreType.DMA((len(SENDS) + 3 * (side - 1),)),
+                pltpu.SemaphoreType.DMA((2,)),
             ],
             compiler_params=pltpu.CompilerParams(collective_id=0, has_side_effects=True),
         )(block_len, span_q, span_kv, cache_kv, anchor_kv, queries, out_weight)

time: 54.9 us -> 52.5 us (0.956)
  Pallas kernels: 52.2 us -> 49.7 us
    pallas_call x1, Pallas kernels: 52.2 us -> 49.7 us  [local(): pl.pallas_call(make_kernel(side, nt, heads), name='star', out_shape=(vmem...]
where the time goes in v3:
time: 52.5 us; the launch traced here: 52.3 us
  Pallas kernels  49.7 us (95%)
  local copies, waits for them, and re-layouts  1.3 us (2%)
  between operations  1.29 us (2%)
    pallas_call x1, Pallas kernels, local(): pl.pallas_call(make_kernel(side, nt, heads), name='star', out_shape=(vmem...  49.7 us
    unnamed x2, local copies, waits for them, and re-layouts  1.3 us

profile of v3, /device:TPU:1, one launch (start us, length us, event | category | flops | bytes accessed | tf_op | source)
XLA Modules:
  0.0 52.3 jit_solution(13778606552452075925)
XLA Ops:
  1.3 49.7 %star.1 = (bf16[128,1024]{1,0:T(8,128)(2,1)S(1)}, bf16[16,128]{1,0:T(8,128)(2,1)S(1)}) custom-call(s32[1]{0:T(128)S(6)} %copy.13.len_hbm, bf16[128,1024]{1,0:T(8,128)(2,1)} %span_q_hbm.1, bf16[2,128,128]{2,1,0:T(8,128)(2,1)} %span_kv_hbm.1, bf16[2,1024,128]{2,1,0:T(8,128)(2,1)} %cache_hbm.1, bf16[2,32,128]{2,1,0:T(8,128)(2,1)} %anchor_hbm.1, ...), custom_call_target="tpu_custom_call" | custom-call | tf_op jit(solution)/shard_map/star/pallas_call | solution.py:437
  51.0 0.7 %copy.11 = bf16[128,1024]{1,0:T(8,128)(2,1)} copy(bf16[128,1024]{1,0:T(8,128)(2,1)S(1)} %get-tuple-element.2) | data formatting | bytes 524288
  51.7 0.6 %copy.12 = bf16[16,128]{1,0:T(8,128)(2,1)} copy(bf16[16,128]{1,0:T(8,128)(2,1)S(1)} %get-tuple-element.3) | data formatting | bytes 8192

commit v4 on v3

--- a/solution.py
+++ b/solution.py
@@ -79,6 +79,7 @@
         b = hi + par * (lo - hi)
 
         other = t + 1 - 2 * par
+        core_one = t + 1 - par
 
         def at(pa, pb, core):
             first = pb * side + pa
@@ -95,6 +96,9 @@
 
         def over_b(k):
             return at(a, lax.rem(b + k, side), other)
+
+        def to_one(k):
+            return at(a, lax.rem(b + k, side), core_one)
 
         def back(x, k):
             return lax.rem(x + side - k, side)
@@ -106,11 +110,13 @@
         first_recv, used = {}, 0
         for x in SENDS:
             first_recv[x] = used
-            used += side if x in single else 1
-
-        def rcopy(src, dst, x, k, dev):
+            used += side if x in single else 2
+
+        second = {CO: len(SENDS), CL: len(SENDS) + 1, GB: len(SENDS) + 2}
+
+        def rcopy(src, dst, x, k, dev, d=0):
             return pltpu.make_async_remote_copy(
-                src_ref=src, dst_ref=dst, send_sem=ss.at[x], recv_sem=rs.at[first_recv[x] + (k if x in single else 0)],
+                src_ref=src, dst_ref=dst, send_sem=ss.at[second[x] if d else x], recv_sem=rs.at[first_recv[x] + k],
                 device_id=dev, device_id_type=MESH,
             )
 
@@ -164,18 +170,20 @@
         def qb(k, owner):
             return rcopy(qx, q_all.at[owner], QB, k, over_a(k))
 
-        def all_of(x, ref):
-            return rcopy(ref, ref, x, 0, over_a(0))
+        def all_of(x, ref, k=0, d=0):
+            return rcopy(ref, ref, x, k, over_a(0), d)
 
         def ab(k, owner):
             place = anc.at[b, :, pl.ds(owner * own_rows, own_rows), :]
-            return rcopy(place, place, AB, k, on_a(k))
+            return rcopy(place, place, AB, 0, on_a(k))
 
         def right(step, slot):
-            return rcopy(anc.at[slot], anc.at[slot], AA, step - 1, on_b(1))
+            place = anc.at[slot] if step < half else anc.at[slot, 0]
+            return rcopy(place, place, AA, step - 1, on_b(1))
 
         def left(step, slot):
-            return rcopy(anc.at[slot], anc.at[slot], AA, half + step - 1, on_b(side - 1))
+            place = anc.at[slot] if step < half else anc.at[slot, 1]
+            return rcopy(place, place, AA, half + step - 1, on_b(side - 1))
 
         def slot_at(offset):
             return lax.rem(b + side + offset, side)
@@ -183,17 +191,19 @@
         def ring_send(step):
             if step <= half:
                 right(step, slot_at(1 - step)).start()
-            if step <= half - 1:
                 left(step, slot_at(step - 1)).start()
 
+        def ring_send_on(core, step):
+            @pl.when(par == core)
+            def _():
+                ring_send(step)
+
         def ring_recv(step):
-            got = []
-            if step <= half:
-                got.append(slot_at(-step))
-                right(step, got[-1]).wait_recv()
-            if step <= half - 1:
-                got.append(slot_at(step))
-                left(step, got[-1]).wait_recv()
+            got = [slot_at(-step), slot_at(step)]
+            right(step, got[0]).wait_recv()
+            left(step, got[1]).wait_recv()
+            if step == half:
+                got = got[:1]
             return got
 
         for k in far_all:
@@ -278,11 +288,11 @@
                 ro_send[owner] = o[i * rows : (i + 1) * rows]
                 rl_send[owner] = as_row(lse[i * rows : (i + 1) * rows])
 
-        def ro_copy(k, block, owner):
-            return rcopy(ro_send.at[block], ro.at[owner], RO, k, over_b(k))
-
-        def rl_copy(k, block, owner):
-            return rcopy(rl_send.at[block], rl.at[owner], RL, k, over_b(k))
+        def ro_copy(k, block):
+            return rcopy(ro_send.at[block], ro.at[par, b], RO, par, to_one(k))
+
+        def rl_copy(k, block):
+            return rcopy(rl_send.at[block], rl.at[par, b], RL, par, to_one(k))
 
         def some_blocks(offsets):
             owners = [back(b, k) for k in offsets]
@@ -290,9 +300,21 @@
                 qb(k, owner).wait_recv()
             query_blocks(owners)
             for k, owner in zip(offsets, owners):
-                k = lax.rem(side - k, side)
-                ro_copy(k, owner, b).start()
-                rl_copy(k, owner, b).start()
+                if isinstance(k, int) and k == 0:
+
+                    @pl.when(par == 1)
+                    def _():
+                        ro[1, b] = ro_send[b]
+                        rl[1, b] = rl_send[b]
+
+                    @pl.when(par == 0)
+                    def _():
+                        ro_copy(0, b).start()
+                        rl_copy(0, b).start()
+
+                else:
+                    ro_copy(side - k, owner).start()
+                    rl_copy(side - k, owner).start()
 
         some_blocks([0])
 
@@ -301,18 +323,21 @@
 
 
         def two_blocks(i, carry):
-            some_blocks([i, side - i])
+            some_blocks([half - i, half + i])
             return carry
 
-        lax.fori_loop(1, half, two_blocks, 0)
+        if half > 1:
+            some_blocks([1, side - 1])
         some_blocks([half])
-
+        lax.fori_loop(1, half - 1, two_blocks, 0)
+
+        slots = [b] + ring_recv(1)
+        ring_send_on(0, 2)
         lax.fori_loop((groups + 1) // 2, groups, first_local, 0)
-        slots = [b] + ring_recv(1)
-        ring_send(2)
-
-        def combine(o_ref, l_ref):
-            lse = [l_ref[i] for i in range(side)]
+        ring_send_on(1, 2)
+
+        def combine(o_ref, l_ref, d):
+            lse = [l_ref[d, i] for i in range(side)]
             peak = lse[0]
             for x in lse[1:]:
                 peak = jnp.maximum(peak, x)
@@ -322,48 +347,74 @@
                 total = total + w
             o = None
             for i in range(side):
-                term = as_col(weights[i] / total) * o_ref[i].astype(jnp.float32)
+                term = as_col(weights[i] / total) * o_ref[d, i].astype(jnp.float32)
                 o = term if o is None else o + term
             return o.astype(jnp.bfloat16), peak + jnp.log2(total)
 
-        all_of(RO, ro).wait_recv()
-        all_of(RL, rl).wait_recv()
-        o, lse = combine(ro, rl)
-        co[b] = o
-        cl[b] = lse
-
-        def co_copy(k, owner):
-            return rcopy(co.at[owner], co.at[owner], CO, k, on_b(k))
-
-        def cl_copy(k, owner):
-            return rcopy(cl.at[owner], cl.at[owner], CL, k, on_b(k))
-
-        for k in far_first:
-            co_copy(k, b).start()
-            cl_copy(k, b).start()
+        def plane_slot(d):
+            return a if d else b
+
+        def plane_peer(d, k):
+            return on_a(k) if d else on_b(k)
+
+        def co_copy(d, k):
+            place = co.at[d, plane_slot(d)]
+            return rcopy(place, place, CO, d, plane_peer(d, k), d)
+
+        def cl_copy(d, k):
+            place = cl.at[d, plane_slot(d)]
+            return rcopy(place, place, CL, d, plane_peer(d, k), d)
+
+        def blocks_of(d):
+            return slice(0, side - 1) if d else slice(0, side)
+
+
+        @pl.when(par == 1)
+        def _():
+            for d in (1, 0):
+                all_of(RO, ro.at[d, blocks_of(d)], d).wait_recv()
+                all_of(RL, rl.at[d, blocks_of(d)], d).wait_recv()
+                o, lse = combine(ro, rl, d)
+                co[d, plane_slot(d)] = o
+                cl[d, plane_slot(d)] = lse
+                for k in far_first:
+                    co_copy(d, k).start()
+                    cl_copy(d, k).start()
 
         if half > 1:
             slots = slots + ring_recv(2)
         first_anchor(slots, last=half <= 2)
         ring_send(3)
 
-        all_of(CO, co.at[0 : side - 1]).wait_recv()
-        all_of(CL, cl.at[0 : side - 1]).wait_recv()
-        o, _ = combine(co, cl)
-        done[...] = o
-
-        def gb(k, owner):
-            return rcopy(done, att.at[owner], GB, k, over_a(k))
-
-        for k in far_all:
-            gb(k, a).start()
+        def gb(d, k):
+            if d:
+                return rcopy(done.at[1], att.at[b], GB, 0, on_b(k), d)
+            return rcopy(done.at[0], att.at[a], GB, 0, over_a(k))
+
+
+        @pl.when(par == 1)
+        def _():
+            for d in (1, 0):
+                all_of(CO, co.at[d, 0 : side - 1], d).wait_recv()
+                all_of(CL, cl.at[d, 0 : side - 1], d).wait_recv()
+                o, _ = combine(co, cl, d)
+                done[d] = o
+                for k in far_first if d else far_all:
+                    gb(d, k).start()
+                if d:
+                    att[b] = o
 
         for step in range(3, half):
             slots = ring_recv(step)
             first_anchor(slots)
             ring_send(step + 1)
 
-        all_of(GB, att).wait_recv()
+        for d in (0, 1):
+
+            @pl.when(par == d)
+            def _():
+                all_of(GB, att.at[blocks_of(d)]).wait_recv()
+
         att_f[...] = att[...].reshape(-1, HD).astype(jnp.float32)
         count = att_f.shape[0] // heads
         per = count // ctx_count
@@ -386,7 +437,7 @@
         tpr[t] = proj[t]
 
         def tp_copy(k, piece, owner):
-            return rcopy(proj.at[piece], tpr.at[owner], TP, k, on_t(k))
+            return rcopy(proj.at[piece], tpr.at[owner], TP, 0, on_t(k))
 
         for k in range(1, nt):
             tp_copy(k, lax.rem(t + k, nt), t).start()
@@ -409,10 +460,23 @@
 
         for x, ref in (
             (QA, qx), (QB, q_all), (AB, anc.at[b, :, pl.ds(0, (side - 1) * own_rows), :]),
-            (AA, anc.at[0 : side - 1]), (RO, ro), (RL, rl), (CO, co.at[0 : side - 1]),
-            (CL, cl.at[0 : side - 1]), (GB, att), (TP, tpr.at[0 : nt - 1]),
+            (AA, anc.at[0 : side - 1]), (TP, tpr.at[0 : nt - 1]),
         ):
             all_of(x, ref).wait_send()
+        for d in (0, 1):
+
+            @pl.when(par == d)
+            def _():
+                all_of(RO, ro_send.at[blocks_of(d)]).wait_send()
+                all_of(RL, rl_send.at[blocks_of(d)]).wait_send()
+
+        @pl.when(par == 1)
+        def _():
+            for d in (0, 1):
+                all_of(CO, co.at[d, 0 : side - 1], d, d).wait_send()
+                all_of(CL, cl.at[d, 0 : side - 1], d, d).wait_send()
+                all_of(GB, att.at[blocks_of(d)], 0, d).wait_send()
+
         store.wait()
         final.wait()
 
@@ -456,11 +520,11 @@
                 vmem((side, 2, side * own, HD), bf16),
                 vmem((side, rows, HD), bf16),
                 vmem((side, 1, rows), f32),
-                vmem((side, rows, HD), bf16),
-                vmem((side, 1, rows), f32),
-                vmem((side, rows, HD), bf16),
-                vmem((side, 1, rows), f32),
-                vmem((rows, HD), bf16),
+                vmem((2, side, rows, HD), bf16),
+                vmem((2, side, 1, rows), f32),
+                vmem((2, side, rows, HD), bf16),
+                vmem((2, side, 1, rows), f32),
+                vmem((2, rows, HD), bf16),
                 vmem((side, rows, HD), bf16),
                 vmem((side * rows, HD), f32),
                 vmem((nt, answer_rows, cols), f32),
@@ -471,8 +535,8 @@
                 vmem(span_q.shape, bf16),
                 vmem((answer_rows, cols), bf16),
                 pltpu.SemaphoreType.DMA((7,)),
-                pltpu.SemaphoreType.DMA((len(SENDS),)),
-                pltpu.SemaphoreType.DMA((len(SENDS) + 3 * (side - 1),)),
+                pltpu.SemaphoreType.DMA((len(SENDS) + 3,)),
+                pltpu.SemaphoreType.DMA((2 * len(SENDS) + 3 * (side - 2),)),
                 pltpu.SemaphoreType.DMA((2,)),
             ],
             compiler_params=pltpu.CompilerParams(collective_id=0, has_side_effects=True),

time: 52.5 us -> 51 us (0.971)
  Pallas kernels: 49.7 us -> 48.2 us
    pallas_call x1, Pallas kernels: 49.7 us -> 48.2 us  [local(): pl.pallas_call(make_kernel(side, nt, heads), name='star', out_shape=(vmem...]
where the time goes in v4:
time: 51 us; the launch traced here: 50.8 us
  Pallas kernels  48.2 us (95%)
  local copies, waits for them, and re-layouts  1.3 us (3%)
  between operations  1.29 us (3%)
    pallas_call x1, Pallas kernels, local(): pl.pallas_call(make_kernel(side, nt, heads), name='star', out_shape=(vmem...  48.2 us
    unnamed x2, local copies, waits for them, and re-layouts  1.3 us

profile of v4, /device:TPU:1, one launch (start us, length us, event | category | flops | bytes accessed | tf_op | source)
XLA Modules:
  0.0 50.8 jit_solution(13070895180536409249)
XLA Ops:
  1.3 48.2 %star.1 = (bf16[128,1024]{1,0:T(8,128)(2,1)S(1)}, bf16[16,128]{1,0:T(8,128)(2,1)S(1)}) custom-call(s32[1]{0:T(128)S(6)} %copy.13.len_hbm, bf16[128,1024]{1,0:T(8,128)(2,1)} %span_q_hbm.1, bf16[2,128,128]{2,1,0:T(8,128)(2,1)} %span_kv_hbm.1, bf16[2,1024,128]{2,1,0:T(8,128)(2,1)} %cache_hbm.1, bf16[2,32,128]{2,1,0:T(8,128)(2,1)} %anchor_hbm.1, ...), custom_call_target="tpu_custom_call" | custom-call | tf_op jit(solution)/shard_map/star/pallas_call | solution.py:501
  49.5 0.7 %copy.11 = bf16[128,1024]{1,0:T(8,128)(2,1)} copy(bf16[128,1024]{1,0:T(8,128)(2,1)S(1)} %get-tuple-element.2) | data formatting | bytes 524288
  50.2 0.6 %copy.12 = bf16[16,128]{1,0:T(8,128)(2,1)} copy(bf16[16,128]{1,0:T(8,128)(2,1)S(1)} %get-tuple-element.3) | data formatting | bytes 8192

commit v5 on v4

--- a/solution.py
+++ b/solution.py
@@ -17,21 +17,6 @@
 
 def scores(q, k):
     return lax.dot_general(q, k, (((1,), (1,)), ((), ())), preferred_element_type=jnp.float32)
-
-
-def softmax_parts(parts, values):
-    peak = None
-    for s in parts:
-        top = jnp.max(s, axis=1, keepdims=True)
-        peak = top if peak is None else jnp.maximum(peak, top)
-    total, out = None, None
-    for s, v in zip(parts, values):
-        w = jnp.exp2((s - peak) * LOG2)
-        part = jnp.sum(w, axis=1, keepdims=True)
-        prod = jnp.dot(w.astype(jnp.bfloat16), v, preferred_element_type=jnp.float32)
-        total = part if total is None else total + part
-        out = prod if out is None else out + prod
-    return peak, total, out
 
 
 def wide(x, columns):
@@ -65,7 +50,7 @@
     def kernel(
         len_hbm, span_q_hbm, span_kv_hbm, cache_hbm, anchor_hbm, queries_hbm, weight_hbm,
         out_any, ans_any,
-        len_ref, span_q, span_kv, cache, anchor, queries, weight, q_rows, bias,
+        len_ref, span_q, kv, queries, weight, q_rows, bias, bias_col, values,
         mine, qx, q_all, anc, ro_send, rl_send, ro, rl, co, cl, done, att, att_f, proj, tpr,
         f_peak, f_sum, f_out, out, ans,
         in_sem, ss, rs, out_sem,
@@ -121,9 +106,13 @@
             )
 
         new_rows = out.shape[0]
+        own_rows = anchor_hbm.shape[1]
+        cached = cache_hbm.shape[1]
+        near = cached + new_rows
+        used = near + own_rows
         pairs = [
-            (queries_hbm, queries), (anchor_hbm, anchor), (len_hbm, len_ref), (cache_hbm, cache),
-            (span_kv_hbm, span_kv), (weight_hbm, weight),
+            (queries_hbm, queries), (anchor_hbm, kv.at[:, near:used]), (len_hbm, len_ref),
+            (cache_hbm, kv.at[:, 0:cached]), (span_kv_hbm, kv.at[:, cached:near]), (weight_hbm, weight),
         ]
         for h in range(heads):
             pairs.append(
@@ -144,17 +133,21 @@
 
         loads[0].wait()
         loads[1].wait()
-        wide = queries[...].astype(jnp.float32)
+        flat = queries[...].astype(jnp.float32)
         for i in range(queries.shape[0]):
             for h in range(heads):
-                q_rows[i * heads + h : i * heads + h + 1, :] = wide[i : i + 1, h * HD : (h + 1) * HD]
+                q_rows[i * heads + h : i * heads + h + 1, :] = flat[i : i + 1, h * HD : (h + 1) * HD]
         mine[...] = q_rows[...].astype(jnp.bfloat16)
-        own_rows = anchor.shape[1]
-        anc[b, :, pl.ds(a * own_rows, own_rows), :] = anchor[...]
+        anc[b, :, pl.ds(a * own_rows, own_rows), :] = kv[:, near:used]
+        if used < kv.shape[1]:
+            kv[:, used:] = jnp.zeros((2, kv.shape[1] - used, HD), jnp.bfloat16)
         loads[2].wait()
         length = len_ref[0]
         column = lax.broadcasted_iota(jnp.int32, bias.shape, 1)
         bias[...] = jnp.where(column < length, 0.0, NEG)
+        column = lax.broadcasted_iota(jnp.int32, bias_col.shape, 0)
+        hidden = ((column >= length) & (column < cached)) | (column >= used)
+        bias_col[...] = jnp.where(hidden, NEG, 0.0)
 
         pl.semaphore_wait(barrier, 4 * (side - 1) + nt - 1)
 
@@ -217,10 +210,10 @@
             r = pl.ds(pl.multiple_of(i * group, group), group)
             q = span_q[r, :]
             parts = [
-                scores(q, cache[0]) + bias[0:1, :],
-                jnp.where(tri_col <= tri_row, scores(q, span_kv[0]), NEG),
+                scores(q, kv[0, 0:cached]) + bias[0:1, :],
+                jnp.where(tri_col <= tri_row, scores(q, kv[0, cached:near]), NEG),
             ]
-            peak, total, o = lane_softmax(parts, [cache[1], span_kv[1]])
+            peak, total, o = lane_softmax(parts, [kv[1, 0:cached], kv[1, cached:near]])
             f_peak[r, :] = peak
             f_sum[r, :] = total
             f_out[r, :] = o
@@ -256,6 +249,7 @@
                 for k in far_all:
                     qb_chunk(k, chunk).start()
 
+        values[...] = kv[1].T
         groups = heads * new_rows // group
         lax.fori_loop(0, (groups + 1) // 2, first_local, 0)
         for k in far_first:
@@ -263,30 +257,20 @@
         forward([0] + sorted({1, side - 1}))
         for d in range(2, half + 1):
             forward(sorted({d, side - d}))
-        diag = lax.broadcasted_iota(jnp.int32, (rows, rows), 0) == lax.broadcasted_iota(
-            jnp.int32, (rows, rows), 1
-        )
-
-        def as_row(col):
-            return jnp.sum(jnp.where(diag, col, 0.0), axis=0, keepdims=True)
-
-        def as_col(row):
-            return jnp.sum(jnp.where(diag, row, 0.0), axis=1, keepdims=True)
-
         def query_blocks(owners):
             q = [q_all[owner].reshape(rows, HD) for owner in owners]
             q = q[0] if len(q) == 1 else jnp.concatenate(q, axis=0)
-            parts = [
-                scores(q, cache[0]) + bias[0:1, :],
-                scores(q, span_kv[0]),
-                scores(q, anchor[0]),
-            ]
-            peak, total, o = softmax_parts(parts, [cache[1], span_kv[1], anchor[1]])
+            count = q.shape[0]
+            w = scores(kv[0], q) + wide(bias_col[:, 0:rows], count)
+            peak = jnp.max(w, axis=0, keepdims=True)
+            w = jnp.exp2((w - peak) * LOG2)
+            total = jnp.sum(w, axis=0, keepdims=True)
+            o = jnp.dot(values[...], w.astype(jnp.bfloat16), preferred_element_type=jnp.float32)
             o = (o / total).astype(jnp.bfloat16)
             lse = peak * LOG2 + jnp.log2(total)
             for i, owner in enumerate(owners):
-                ro_send[owner] = o[i * rows : (i + 1) * rows]
-                rl_send[owner] = as_row(lse[i * rows : (i + 1) * rows])
+                ro_send[owner] = o[:, i * rows : (i + 1) * rows]
+                rl_send[owner] = lse[:, i * rows : (i + 1) * rows]
 
         def ro_copy(k, block):
             return rcopy(ro_send.at[block], ro.at[par, b], RO, par, to_one(k))
@@ -335,6 +319,11 @@
         ring_send_on(0, 2)
         lax.fori_loop((groups + 1) // 2, groups, first_local, 0)
         ring_send_on(1, 2)
+
+
+        @pl.when(par == 0)
+        def _():
+            first_anchor(slots, last=half == 1)
 
         def combine(o_ref, l_ref, d):
             lse = [l_ref[d, i] for i in range(side)]
@@ -347,9 +336,9 @@
                 total = total + w
             o = None
             for i in range(side):
-                term = as_col(weights[i] / total) * o_ref[d, i].astype(jnp.float32)
+                term = (weights[i] / total) * o_ref[d, i].astype(jnp.float32)
                 o = term if o is None else o + term
-            return o.astype(jnp.bfloat16), peak + jnp.log2(total)
+            return o, peak + jnp.log2(total)
 
         def plane_slot(d):
             return a if d else b
@@ -375,15 +364,23 @@
                 all_of(RO, ro.at[d, blocks_of(d)], d).wait_recv()
                 all_of(RL, rl.at[d, blocks_of(d)], d).wait_recv()
                 o, lse = combine(ro, rl, d)
-                co[d, plane_slot(d)] = o
+                co[d, plane_slot(d)] = o.astype(jnp.bfloat16)
                 cl[d, plane_slot(d)] = lse
                 for k in far_first:
                     co_copy(d, k).start()
                     cl_copy(d, k).start()
 
-        if half > 1:
-            slots = slots + ring_recv(2)
-        first_anchor(slots, last=half <= 2)
+        more = ring_recv(2) if half > 1 else []
+        if more:
+
+            @pl.when(par == 0)
+            def _():
+                first_anchor(more, last=half == 2)
+
+        @pl.when(par == 1)
+        def _():
+            first_anchor(slots + more, last=half <= 2)
+
         ring_send(3)
 
         def gb(d, k):
@@ -398,6 +395,7 @@
                 all_of(CO, co.at[d, 0 : side - 1], d).wait_recv()
                 all_of(CL, cl.at[d, 0 : side - 1], d).wait_recv()
                 o, _ = combine(co, cl, d)
+                o = o.T.astype(jnp.bfloat16)
                 done[d] = o
                 for k in far_first if d else far_all:
                     gb(d, k).start()
@@ -483,6 +481,17 @@
     return kernel
 
 
+def write_out(out_ref, ans_ref, out_hbm, ans_hbm, sem):
+    copies = [
+        pltpu.make_async_copy(out_ref, out_hbm, sem.at[0]),
+        pltpu.make_async_copy(ans_ref, ans_hbm, sem.at[1]),
+    ]
+    for copy in copies:
+        copy.start()
+    for copy in copies:
+        copy.wait()
+
+
 def make_local(ctx_count, nt):
     side = math.isqrt(ctx_count)
 
@@ -494,11 +503,12 @@
         rows = side * chunk
         own = anchor_kv.shape[1]
         cols = out_weight.shape[1]
+        keys = pl.cdiv(cache_kv.shape[1] + new_rows + own, HD) * HD
         answer_rows = per * ctx_count // nt
         any_spec = pl.BlockSpec(memory_space=pl.ANY)
         bf16, f32 = jnp.bfloat16, jnp.float32
         vmem = pltpu.VMEM
-        return pl.pallas_call(
+        results = pl.pallas_call(
             make_kernel(side, nt, heads),
             name="star",
             out_shape=(vmem(span_q.shape, bf16), vmem((answer_rows, cols), bf16)),
@@ -507,22 +517,22 @@
             scratch_shapes=[
                 pltpu.SMEM(block_len.shape, jnp.int32),
                 vmem((heads * new_rows, HD), bf16),
-                vmem(span_kv.shape, bf16),
-                vmem(cache_kv.shape, bf16),
-                vmem(anchor_kv.shape, bf16),
+                vmem((2, keys, HD), bf16),
                 vmem(queries.shape, bf16),
                 vmem(out_weight.shape, bf16),
                 vmem((chunk, HD), f32),
                 vmem((8, cache_kv.shape[1]), f32),
+                vmem((keys, HD), f32),
+                vmem((HD, keys), bf16),
                 vmem((chunk, HD), bf16),
                 vmem((side, chunk, HD), bf16),
                 vmem((side, side, chunk, HD), bf16),
                 vmem((side, 2, side * own, HD), bf16),
-                vmem((side, rows, HD), bf16),
+                vmem((side, HD, rows), bf16),
                 vmem((side, 1, rows), f32),
-                vmem((2, side, rows, HD), bf16),
+                vmem((2, side, HD, rows), bf16),
                 vmem((2, side, 1, rows), f32),
-                vmem((2, side, rows, HD), bf16),
+                vmem((2, side, HD, rows), bf16),
                 vmem((2, side, 1, rows), f32),
                 vmem((2, rows, HD), bf16),
                 vmem((side, rows, HD), bf16),
@@ -541,6 +551,14 @@
             ],
             compiler_params=pltpu.CompilerParams(collective_id=0, has_side_effects=True),
         )(block_len, span_q, span_kv, cache_kv, anchor_kv, queries, out_weight)
+        return pl.pallas_call(
+            write_out,
+            name="write",
+            out_shape=[jax.ShapeDtypeStruct(x.shape, x.dtype) for x in results],
+            in_specs=[pl.BlockSpec(memory_space=pltpu.VMEM)] * 2,
+            out_specs=[any_spec, any_spec],
+            scratch_shapes=[pltpu.SemaphoreType.DMA((2,))],
+        )(*[pltpu.with_memory_space_constraint(x, pltpu.VMEM) for x in results])
 
     return local
 

time: 51 us -> 50.5 us (level)
  local copies, waits for them, and re-layouts: 1.3 us -> 0 us
  Pallas kernels: 48.2 us -> 49.1 us
    unnamed x2 -> x0, local copies, waits for them, and re-layouts: 1.3 us -> none
    pallas_call x0 -> x1, Pallas kernels: none -> 0.72 us  [local(): pl.pallas_call(write_out, name='write', out_shape=[jax.ShapeDtypeStruct(x...]
where the time goes in v5:
time: 50.5 us; the launch traced here: 50.3 us
  Pallas kernels  49.1 us (97%)
  between operations  1.29 us (3%)
    pallas_call x1, Pallas kernels, local(): pl.pallas_call(make_kernel(side, nt, heads), name='star', out_shape=(vmem...  48.3 us

profile of v5, /device:TPU:1, one launch (start us, length us, event | category | flops | bytes accessed | tf_op | source)
XLA Modules:
  0.0 50.3 jit_solution(14422192628199514472)
XLA Ops:
  1.3 48.3 %star.1 = (bf16[128,1024]{1,0:T(8,128)(2,1)S(1)}, bf16[16,128]{1,0:T(8,128)(2,1)S(1)}) custom-call(s32[1]{0:T(128)S(6)} %copy.9.len_hbm, bf16[128,1024]{1,0:T(8,128)(2,1)} %span_q_hbm.1, bf16[2,128,128]{2,1,0:T(8,128)(2,1)} %span_kv_hbm.1, bf16[2,1024,128]{2,1,0:T(8,128)(2,1)} %cache_hbm.1, bf16[2,32,128]{2,1,0:T(8,128)(2,1)} %anchor_hbm.1, ...), custom_call_target="tpu_custom_call" | custom-call | tf_op jit(solution)/shard_map/star/pallas_call | solution.py:511
  49.6 0.7 %write.1 = (bf16[128,1024]{1,0:T(8,128)(2,1)}, bf16[16,128]{1,0:T(8,128)(2,1)}) custom-call(bf16[128,1024]{1,0:T(8,128)(2,1)S(1)} %get-tuple-element.4.out_ref, bf16[16,128]{1,0:T(8,128)(2,1)S(1)} %get-tuple-element.5.ans_ref), custom_call_target="tpu_custom_call" | custom-call | tf_op jit(solution)/shard_map/write/pallas_call | solution.py:554

commit v6 on v5

--- a/solution.py
+++ b/solution.py
@@ -391,7 +391,7 @@
 
         @pl.when(par == 1)
         def _():
-            for d in (1, 0):
+            for d in (0, 1):
                 all_of(CO, co.at[d, 0 : side - 1], d).wait_recv()
                 all_of(CL, cl.at[d, 0 : side - 1], d).wait_recv()
                 o, _ = combine(co, cl, d)
@@ -415,30 +415,29 @@
 
         att_f[...] = att[...].reshape(-1, HD).astype(jnp.float32)
         count = att_f.shape[0] // heads
-        per = count // ctx_count
-        row = lax.broadcasted_iota(jnp.int32, (count, count), 0)
-        col = lax.broadcasted_iota(jnp.int32, (count, count), 1)
-        dev, sub = lax.div(row, per), lax.rem(row, per)
-        swapped = (lax.rem(dev, side) * side + lax.div(dev, side)) * per + sub
-        source = row + par * (swapped - row)
-        perm = jnp.where(col == source, 1.0, 0.0).astype(jnp.bfloat16)
         total = None
         for h in range(heads):
             rows_h = att_f[pl.ds(h, count, stride=heads), :].astype(jnp.bfloat16)
-            rows_h = jnp.dot(perm, rows_h, preferred_element_type=jnp.float32)
             term = jnp.dot(
-                rows_h.astype(jnp.bfloat16), weight[h * HD : (h + 1) * HD, :],
-                preferred_element_type=jnp.float32,
+                rows_h, weight[h * HD : (h + 1) * HD, :], preferred_element_type=jnp.float32
             )
             total = term if total is None else total + term
         proj[...] = total.reshape(proj.shape)
-        tpr[t] = proj[t]
-
-        def tp_copy(k, piece, owner):
-            return rcopy(proj.at[piece], tpr.at[owner], TP, 0, on_t(k))
-
-        for k in range(1, nt):
-            tp_copy(k, lax.rem(t + k, nt), t).start()
+
+        for d in (0, 1):
+
+            @pl.when(par == d)
+            def _():
+                tpr[t] = proj[:, t] if d else proj[t]
+
+        for d in (0, 1):
+
+            @pl.when(par == d)
+            def _():
+                for k in range(1, nt):
+                    piece = lax.rem(t + k, nt)
+                    piece = proj.at[:, piece] if d else proj.at[piece]
+                    rcopy(piece, tpr.at[t], TP, 0, on_t(k)).start()
 
         if half > 2:
             slots = ring_recv(half)
@@ -452,7 +451,7 @@
         total = tpr[0]
         for i in range(1, nt):
             total = total + tpr[i]
-        ans[...] = total.astype(jnp.bfloat16)
+        ans[...] = total.reshape(ans.shape).astype(jnp.bfloat16)
         final = pltpu.make_async_copy(ans, ans_any, out_sem.at[1])
         final.start()
 
@@ -537,8 +536,8 @@
                 vmem((2, rows, HD), bf16),
                 vmem((side, rows, HD), bf16),
                 vmem((side * rows, HD), f32),
-                vmem((nt, answer_rows, cols), f32),
-                vmem((nt, answer_rows, cols), f32),
+                vmem((side, side, per, cols), f32),
+                vmem((nt, side, per, cols), f32),
                 vmem((heads * new_rows, HD), f32),
                 vmem((heads * new_rows, HD), f32),
                 vmem((heads * new_rows, HD), f32),

time: 50.5 us -> 50.1 us (level)
  no operation moved by 1% of the time
where the time goes in v6:
time: 50.1 us; the launch traced here: 49.9 us
  Pallas kernels  48.6 us (97%)
  between operations  1.29 us (3%)
    pallas_call x1, Pallas kernels, local(): pl.pallas_call(make_kernel(side, nt, heads), name='star', out_shape=(vmem...  47.9 us

profile of v6, /device:TPU:1, one launch (start us, length us, event | category | flops | bytes accessed | tf_op | source)
XLA Modules:
  0.0 49.9 jit_solution(102307459902809057)
XLA Ops:
  1.3 47.9 %star.1 = (bf16[128,1024]{1,0:T(8,128)(2,1)S(1)}, bf16[16,128]{1,0:T(8,128)(2,1)S(1)}) custom-call(s32[1]{0:T(128)S(6)} %copy.9.len_hbm, bf16[128,1024]{1,0:T(8,128)(2,1)} %span_q_hbm.1, bf16[2,128,128]{2,1,0:T(8,128)(2,1)} %span_kv_hbm.1, bf16[2,1024,128]{2,1,0:T(8,128)(2,1)} %cache_hbm.1, bf16[2,32,128]{2,1,0:T(8,128)(2,1)} %anchor_hbm.1, ...), custom_call_target="tpu_custom_call" | custom-call | tf_op jit(solution)/shard_map/star/pallas_call | solution.py:510
  49.2 0.7 %write.1 = (bf16[128,1024]{1,0:T(8,128)(2,1)}, bf16[16,128]{1,0:T(8,128)(2,1)}) custom-call(bf16[128,1024]{1,0:T(8,128)(2,1)S(1)} %get-tuple-element.4.out_ref, bf16[16,128]{1,0:T(8,128)(2,1)S(1)} %get-tuple-element.5.ans_ref), custom_call_target="tpu_custom_call" | custom-call | tf_op jit(solution)/shard_map/write/pallas_call | solution.py:553

commit v7 on v6

--- a/solution.py
+++ b/solution.py
@@ -95,7 +95,7 @@
         first_recv, used = {}, 0
         for x in SENDS:
             first_recv[x] = used
-            used += side if x in single else 2
+            used += side if x in single else 2 if x in (RO, RL, CO, CL) else 1
 
         second = {CO: len(SENDS), CL: len(SENDS) + 1, GB: len(SENDS) + 2}
 
@@ -306,14 +306,12 @@
         ring_send(1)
 
 
-        def two_blocks(i, carry):
-            some_blocks([half - i, half + i])
-            return carry
-
         if half > 1:
             some_blocks([1, side - 1])
         some_blocks([half])
-        lax.fori_loop(1, half - 1, two_blocks, 0)
+        rest = [k for i in range(1, half - 1) for k in (half - i, half + i)]
+        if rest:
+            some_blocks(rest)
 
         slots = [b] + ring_recv(1)
         ring_send_on(0, 2)
@@ -545,7 +543,7 @@
                 vmem((answer_rows, cols), bf16),
                 pltpu.SemaphoreType.DMA((7,)),
                 pltpu.SemaphoreType.DMA((len(SENDS) + 3,)),
-                pltpu.SemaphoreType.DMA((2 * len(SENDS) + 3 * (side - 2),)),
+                pltpu.SemaphoreType.DMA((len(SENDS) + 4 + 3 * (side - 1),)),
                 pltpu.SemaphoreType.DMA((2,)),
             ],
             compiler_params=pltpu.CompilerParams(collective_id=0, has_side_effects=True),

time: 50.1 us -> 50.3 us (level)
  no operation moved by 1% of the time
where the time goes in v7:
time: 50.3 us; the launch traced here: 50.1 us
  Pallas kernels  48.9 us (97%)
  between operations  1.29 us (3%)
    pallas_call x1, Pallas kernels, local(): pl.pallas_call(make_kernel(side, nt, heads), name='star', out_shape=(vmem...  48.1 us

profile of v7, /device:TPU:1, one launch (start us, length us, event | category | flops | bytes accessed | tf_op | source)
XLA Modules:
  0.0 50.1 jit_solution(4864919098847092430)
XLA Ops:
  1.3 48.1 %star.1 = (bf16[128,1024]{1,0:T(8,128)(2,1)S(1)}, bf16[16,128]{1,0:T(8,128)(2,1)S(1)}) custom-call(s32[1]{0:T(128)S(6)} %copy.9.len_hbm, bf16[128,1024]{1,0:T(8,128)(2,1)} %span_q_hbm.1, bf16[2,128,128]{2,1,0:T(8,128)(2,1)} %span_kv_hbm.1, bf16[2,1024,128]{2,1,0:T(8,128)(2,1)} %cache_hbm.1, bf16[2,32,128]{2,1,0:T(8,128)(2,1)} %anchor_hbm.1, ...), custom_call_target="tpu_custom_call" | custom-call | tf_op jit(solution)/shard_map/star/pallas_call | solution.py:508
  49.4 0.7 %write.1 = (bf16[128,1024]{1,0:T(8,128)(2,1)}, bf16[16,128]{1,0:T(8,128)(2,1)}) custom-call(bf16[128,1024]{1,0:T(8,128)(2,1)S(1)} %get-tuple-element.4.out_ref, bf16[16,128]{1,0:T(8,128)(2,1)S(1)} %get-tuple-element.5.ans_ref), custom_call_target="tpu_custom_call" | custom-call | tf_op jit(solution)/shard_map/write/pallas_call | solution.py:551
